TPU v7x, 256 devices: a whole 4x4x8 slice. The times are simulated.
256 devices in a mesh: pp: 2 (over y_hi), cp: 32 (over x, z), tp: 4 (over y_lo, core).
Axes of the slice: x: 4, y: 4 (y_hi: 2, y_lo: 2; y = y_hi * 2 + y_lo), z: 8, core: 2. Of those that a mesh axis runs over, the one named last changes fastest.
Arguments:
- queries: bfloat16 [2, 4096, 8192], P('pp', 'cp', 'tp'), may hold values from -9 to 9
- key_vectors: bfloat16 [2, 4096, 512], P('pp', 'cp', 'tp'), may hold values from -6 to 6
- value_vectors: bfloat16 [2, 4096, 512], P('pp', 'cp', 'tp'), may hold values from -30 to 30
- block_order: int32 [64], replicated, may hold values from 0 to 63, each once
- norm_gain: bfloat16 [2, 8192], P('pp', 'tp'), may hold values from 0.099609375 to 1.8984375
- kv_weight: bfloat16 [2, 8192, 1024], P('pp', 'tp'), may hold values from -0.0625 to 0.0625
Outputs:
- max_logits: float32 [2, 64], P('pp', 'tp')
- kv_next: bfloat16 [2, 4096, 1024], P('pp', 'cp', 'tp')
Inputs may be any that keep to these rules, and one draw needn't show every extreme that they name: A permutation; rows 2 c * 64 to (2 c + 2) * 64 - 1 hold the positions of blocks block_order[2 c] and block_order[2 c + 1], in that order.
All inputs are finite; a program needn't handle non-finite values.
Results may differ from a plain program's by a relative error of at most 0.018.
Values may be sent and summed in bfloat16 or wider, within the bound.
A program may use at most 128 MiB of HBM per device.

v0:
```python
import math

import jax
import jax.numpy as jnp
from jax import lax
from jax.sharding import PartitionSpec as P

DH = 128


floor_value = -1e30


def shifted(block, axis, distance):
    devices = range(lax.axis_size(axis))
    route = [((i - distance) % len(devices), i) for i in devices]
    return lax.ppermute(block, axis, route)


def on_device(queries, key_vectors, value_vectors, block_order, norm_gain, kv_weight):
    axis_size = lax.axis_size("cp")
    my_index = lax.axis_index("cp")
    tok_rows = queries.shape[1]
    block_rows = tok_rows // 2
    kv_local = key_vectors.shape[2] // DH
    heads_local = queries.shape[2] // DH
    group_size = heads_local // kv_local
    score_scale = 1.0 / math.sqrt(DH)
    query_block = queries[0].reshape(tok_rows, kv_local, group_size, DH)
    slot_ids = jnp.arange(2 * axis_size, dtype=jnp.int32)

    def positions(first_row, row_count):
        row_ids = first_row + jnp.arange(row_count, dtype=jnp.int32)
        member = (row_ids // block_rows)[:, None] == slot_ids[None, :]
        block_ids = jnp.sum(jnp.where(member, block_order[None, :], 0), axis=1)
        return block_ids * block_rows + row_ids % block_rows

    query_pos = positions(my_index * tok_rows, tok_rows)

    def attend(carry_state, key_pair, key_pos):
        running_max, running_sum, weighted = carry_state
        k_part = key_pair[0].reshape(-1, kv_local, DH)
        v_part = key_pair[1].reshape(-1, kv_local, DH)
        scores = (
            jnp.einsum("tkgd,skd->tkgs", query_block, k_part, preferred_element_type=jnp.float32)
            * score_scale
        )
        allowed = (key_pos[None, :] <= query_pos[:, None])[:, None, None, :]
        masked = jnp.where(allowed, scores, floor_value)
        new_max = jnp.maximum(running_max, jnp.max(masked, axis=3))
        weights = jnp.where(allowed, jnp.exp(masked - new_max[..., None]), 0.0)
        shrink = jnp.exp(running_max - new_max)
        running_sum = running_sum * shrink + jnp.sum(weights, axis=3)
        update = jnp.einsum(
            "tkgs,skd->tkgd",
            weights.astype(jnp.bfloat16),
            v_part,
            preferred_element_type=jnp.float32,
        )
        weighted = weighted * shrink[..., None] + update
        return (new_max, running_sum, weighted)

    def consider(carry_state, key_pair, key_pos):
        return attend(carry_state, key_pair, key_pos)

    initial = (
        jnp.full((tok_rows, kv_local, group_size), floor_value, jnp.float32),
        jnp.zeros((tok_rows, kv_local, group_size), jnp.float32),
        jnp.zeros((tok_rows, kv_local, group_size, DH), jnp.float32),
    )
    key_pair = jnp.stack([key_vectors[0], value_vectors[0]])
    opening = consider(initial, key_pair, query_pos)

    def advance(turn_index, carry):
        carry_state, moving = carry
        moving = shifted(moving, "cp", 1)
        source = (my_index - turn_index) % axis_size
        return (consider(carry_state, moving, positions(source * tok_rows, tok_rows)), moving)

    finished, moving = lax.fori_loop(1, axis_size, advance, (opening, key_pair))
    running_max, running_sum, weighted = finished
    context = (
        (weighted / running_sum[..., None]).reshape(tok_rows, heads_local * DH).astype(jnp.bfloat16)
    )
    local_peak = jnp.max(running_max, axis=0)
    max_logits = lax.pmax(local_peak, "cp")
    handed = shifted(context, "pp", 1)
    wide = handed.astype(jnp.float32)
    squares = lax.psum(jnp.sum(wide * wide, axis=1), "tp")
    features = heads_local * DH * lax.axis_size("tp")
    inverse = lax.rsqrt(squares / features + 1e-05)
    normed = (wide * inverse[:, None] * norm_gain[0].astype(jnp.float32)[None, :]).astype(
        jnp.bfloat16
    )
    partial_sums = jnp.dot(normed, kv_weight[0], preferred_element_type=jnp.float32)
    kv_next = lax.psum_scatter(
        partial_sums.astype(jnp.bfloat16), "tp", scatter_dimension=1, tiled=True
    )
    return (max_logits, kv_next[None])


def solution(mesh):
    return jax.shard_map(
        on_device,
        mesh=mesh,
        in_specs=(
            P("pp", "cp", "tp"),
            P("pp", "cp", "tp"),
            P("pp", "cp", "tp"),
            P(),
            P("pp", "tp"),
            P("pp", "tp", None),
        ),
        out_specs=(P("pp", "tp"), P("pp", "cp", "tp")),
        check_vma=False,
    )
```

profile of v0, /device:TPU:8, one launch (start us, length us, event | category | flops | bytes accessed | tf_op | source)
XLA Modules:
  0.0 393.6 jit_solution(11747659148686527185)
XLA Ops:
  7.3 0.7 select_reduce_fusion.1
  8.1 1.3 copy.20
  9.4 1.1 copy.25
  10.6 1.1 fusion.45
  11.7 0.8 pad_maximum_fusion
  13.5 281.5 %while.23 = (s32[]{:T(128)}, f32[128,1,16]{0,2,1:T(8,128)S(1)}, f32[128,1,16]{0,2,1:T(8,128)S(1)}, f32[128,1,16,128]{3,0,2,1:T(8,128)S(1)}, bf16[2,128,128]{2,1,...) while((s32[]{:T(128)}, f32[128,1,16]{0,2,1:T(8,128)S(1)}, ...), condition=%wide.region_7.8_spmd.clone, body=%wide.region_3.7_spmd.clone.sunk | while | flops 137152144 | bytes 6426682 | solution.py:80
  13.5 2.0 collective-permute-start
  15.7 8.2 %collective-permute-done = bf16[2,128,128]{2,1,0:T(8,128)(2,1)S(1)} collective-permute-done((bf16[2,128,128]{2,1,0:T(8,128)(2,1)S(1)}, bf16[2,128,128]{2,1,0:T(8,128)(2,1)S(1)}, u32[]{:S(2)}, u32[]{:S(2)}) %collective-permute-start) | collective-permute-done | bytes 65568 | tf_op jit(solution)/shard_map/while/body/eval_jaxpr/ppermute | solution.py:17
  25.5 7.3 %collective-permute-done = bf16[2,128,128]{2,1,0:T(8,128)(2,1)S(1)} collective-permute-done((bf16[2,128,128]{2,1,0:T(8,128)(2,1)S(1)}, bf16[2,128,128]{2,1,0:T(8,128)(2,1)S(1)}, u32[]{:S(2)}, u32[]{:S(2)}) %collective-permute-start) | collective-permute-done | bytes 65568 | tf_op jit(solution)/shard_map/while/body/eval_jaxpr/ppermute | solution.py:17
  33.4 0.7 fusion.57
  34.4 7.3 %collective-permute-done = bf16[2,128,128]{2,1,0:T(8,128)(2,1)S(1)} collective-permute-done((bf16[2,128,128]{2,1,0:T(8,128)(2,1)S(1)}, bf16[2,128,128]{2,1,0:T(8,128)(2,1)S(1)}, u32[]{:S(2)}, u32[]{:S(2)}) %collective-permute-start) | collective-permute-done | bytes 65568 | tf_op jit(solution)/shard_map/while/body/eval_jaxpr/ppermute | solution.py:17
  42.3 0.7 fusion.57
  43.4 7.3 %collective-permute-done = bf16[2,128,128]{2,1,0:T(8,128)(2,1)S(1)} collective-permute-done((bf16[2,128,128]{2,1,0:T(8,128)(2,1)S(1)}, bf16[2,128,128]{2,1,0:T(8,128)(2,1)S(1)}, u32[]{:S(2)}, u32[]{:S(2)}) %collective-permute-start) | collective-permute-done | bytes 65568 | tf_op jit(solution)/shard_map/while/body/eval_jaxpr/ppermute | solution.py:17
  51.3 0.7 fusion.57
  52.3 7.3 %collective-permute-done = bf16[2,128,128]{2,1,0:T(8,128)(2,1)S(1)} collective-permute-done((bf16[2,128,128]{2,1,0:T(8,128)(2,1)S(1)}, bf16[2,128,128]{2,1,0:T(8,128)(2,1)S(1)}, u32[]{:S(2)}, u32[]{:S(2)}) %collective-permute-start) | collective-permute-done | bytes 65568 | tf_op jit(solution)/shard_map/while/body/eval_jaxpr/ppermute | solution.py:17
  60.2 0.7 fusion.57
  61.2 7.3 %collective-permute-done = bf16[2,128,128]{2,1,0:T(8,128)(2,1)S(1)} collective-permute-done((bf16[2,128,128]{2,1,0:T(8,128)(2,1)S(1)}, bf16[2,128,128]{2,1,0:T(8,128)(2,1)S(1)}, u32[]{:S(2)}, u32[]{:S(2)}) %collective-permute-start) | collective-permute-done | bytes 65568 | tf_op jit(solution)/shard_map/while/body/eval_jaxpr/ppermute | solution.py:17
  69.1 0.7 fusion.57
  70.1 8.0 %collective-permute-done = bf16[2,128,128]{2,1,0:T(8,128)(2,1)S(1)} collective-permute-done((bf16[2,128,128]{2,1,0:T(8,128)(2,1)S(1)}, bf16[2,128,128]{2,1,0:T(8,128)(2,1)S(1)}, u32[]{:S(2)}, u32[]{:S(2)}) %collective-permute-start) | collective-permute-done | bytes 65568 | tf_op jit(solution)/shard_map/while/body/eval_jaxpr/ppermute | solution.py:17
  78.7 0.7 fusion.57
  79.7 7.3 %collective-permute-done = bf16[2,128,128]{2,1,0:T(8,128)(2,1)S(1)} collective-permute-done((bf16[2,128,128]{2,1,0:T(8,128)(2,1)S(1)}, bf16[2,128,128]{2,1,0:T(8,128)(2,1)S(1)}, u32[]{:S(2)}, u32[]{:S(2)}) %collective-permute-start) | collective-permute-done | bytes 65568 | tf_op jit(solution)/shard_map/while/body/eval_jaxpr/ppermute | solution.py:17
  87.7 0.7 fusion.57
  88.7 7.3 %collective-permute-done = bf16[2,128,128]{2,1,0:T(8,128)(2,1)S(1)} collective-permute-done((bf16[2,128,128]{2,1,0:T(8,128)(2,1)S(1)}, bf16[2,128,128]{2,1,0:T(8,128)(2,1)S(1)}, u32[]{:S(2)}, u32[]{:S(2)}) %collective-permute-start) | collective-permute-done | bytes 65568 | tf_op jit(solution)/shard_map/while/body/eval_jaxpr/ppermute | solution.py:17
  96.6 0.7 fusion.57
  97.6 7.3 %collective-permute-done = bf16[2,128,128]{2,1,0:T(8,128)(2,1)S(1)} collective-permute-done((bf16[2,128,128]{2,1,0:T(8,128)(2,1)S(1)}, bf16[2,128,128]{2,1,0:T(8,128)(2,1)S(1)}, u32[]{:S(2)}, u32[]{:S(2)}) %collective-permute-start) | collective-permute-done | bytes 65568 | tf_op jit(solution)/shard_map/while/body/eval_jaxpr/ppermute | solution.py:17
  105.5 0.7 fusion.57
  106.5 7.3 %collective-permute-done = bf16[2,128,128]{2,1,0:T(8,128)(2,1)S(1)} collective-permute-done((bf16[2,128,128]{2,1,0:T(8,128)(2,1)S(1)}, bf16[2,128,128]{2,1,0:T(8,128)(2,1)S(1)}, u32[]{:S(2)}, u32[]{:S(2)}) %collective-permute-start) | collective-permute-done | bytes 65568 | tf_op jit(solution)/shard_map/while/body/eval_jaxpr/ppermute | solution.py:17
  114.4 0.7 fusion.57
  115.4 7.3 %collective-permute-done = bf16[2,128,128]{2,1,0:T(8,128)(2,1)S(1)} collective-permute-done((bf16[2,128,128]{2,1,0:T(8,128)(2,1)S(1)}, bf16[2,128,128]{2,1,0:T(8,128)(2,1)S(1)}, u32[]{:S(2)}, u32[]{:S(2)}) %collective-permute-start) | collective-permute-done | bytes 65568 | tf_op jit(solution)/shard_map/while/body/eval_jaxpr/ppermute | solution.py:17
  123.4 0.7 fusion.57
  124.4 7.3 %collective-permute-done = bf16[2,128,128]{2,1,0:T(8,128)(2,1)S(1)} collective-permute-done((bf16[2,128,128]{2,1,0:T(8,128)(2,1)S(1)}, bf16[2,128,128]{2,1,0:T(8,128)(2,1)S(1)}, u32[]{:S(2)}, u32[]{:S(2)}) %collective-permute-start) | collective-permute-done | bytes 65568 | tf_op jit(solution)/shard_map/while/body/eval_jaxpr/ppermute | solution.py:17
  132.3 0.7 fusion.57
  133.3 8.0 %collective-permute-done = bf16[2,128,128]{2,1,0:T(8,128)(2,1)S(1)} collective-permute-done((bf16[2,128,128]{2,1,0:T(8,128)(2,1)S(1)}, bf16[2,128,128]{2,1,0:T(8,128)(2,1)S(1)}, u32[]{:S(2)}, u32[]{:S(2)}) %collective-permute-start) | collective-permute-done | bytes 65568 | tf_op jit(solution)/shard_map/while/body/eval_jaxpr/ppermute | solution.py:17
  142.9 7.3 %collective-permute-done = bf16[2,128,128]{2,1,0:T(8,128)(2,1)S(1)} collective-permute-done((bf16[2,128,128]{2,1,0:T(8,128)(2,1)S(1)}, bf16[2,128,128]{2,1,0:T(8,128)(2,1)S(1)}, u32[]{:S(2)}, u32[]{:S(2)}) %collective-permute-start) | collective-permute-done | bytes 65568 | tf_op jit(solution)/shard_map/while/body/eval_jaxpr/ppermute | solution.py:17
  150.8 0.7 fusion.57
  151.8 7.3 %collective-permute-done = bf16[2,128,128]{2,1,0:T(8,128)(2,1)S(1)} collective-permute-done((bf16[2,128,128]{2,1,0:T(8,128)(2,1)S(1)}, bf16[2,128,128]{2,1,0:T(8,128)(2,1)S(1)}, u32[]{:S(2)}, u32[]{:S(2)}) %collective-permute-start) | collective-permute-done | bytes 65568 | tf_op jit(solution)/shard_map/while/body/eval_jaxpr/ppermute | solution.py:17
  159.8 0.7 fusion.57
  160.8 7.3 %collective-permute-done = bf16[2,128,128]{2,1,0:T(8,128)(2,1)S(1)} collective-permute-done((bf16[2,128,128]{2,1,0:T(8,128)(2,1)S(1)}, bf16[2,128,128]{2,1,0:T(8,128)(2,1)S(1)}, u32[]{:S(2)}, u32[]{:S(2)}) %collective-permute-start) | collective-permute-done | bytes 65568 | tf_op jit(solution)/shard_map/while/body/eval_jaxpr/ppermute | solution.py:17
  168.7 0.7 fusion.57
  169.7 7.3 %collective-permute-done = bf16[2,128,128]{2,1,0:T(8,128)(2,1)S(1)} collective-permute-done((bf16[2,128,128]{2,1,0:T(8,128)(2,1)S(1)}, bf16[2,128,128]{2,1,0:T(8,128)(2,1)S(1)}, u32[]{:S(2)}, u32[]{:S(2)}) %collective-permute-start) | collective-permute-done | bytes 65568 | tf_op jit(solution)/shard_map/while/body/eval_jaxpr/ppermute | solution.py:17
  177.6 0.7 fusion.57
  178.6 7.3 %collective-permute-done = bf16[2,128,128]{2,1,0:T(8,128)(2,1)S(1)} collective-permute-done((bf16[2,128,128]{2,1,0:T(8,128)(2,1)S(1)}, bf16[2,128,128]{2,1,0:T(8,128)(2,1)S(1)}, u32[]{:S(2)}, u32[]{:S(2)}) %collective-permute-start) | collective-permute-done | bytes 65568 | tf_op jit(solution)/shard_map/while/body/eval_jaxpr/ppermute | solution.py:17
  187.5 7.3 %collective-permute-done = bf16[2,128,128]{2,1,0:T(8,128)(2,1)S(1)} collective-permute-done((bf16[2,128,128]{2,1,0:T(8,128)(2,1)S(1)}, bf16[2,128,128]{2,1,0:T(8,128)(2,1)S(1)}, u32[]{:S(2)}, u32[]{:S(2)}) %collective-permute-start) | collective-permute-done | bytes 65568 | tf_op jit(solution)/shard_map/while/body/eval_jaxpr/ppermute | solution.py:17
  196.5 8.0 %collective-permute-done = bf16[2,128,128]{2,1,0:T(8,128)(2,1)S(1)} collective-permute-done((bf16[2,128,128]{2,1,0:T(8,128)(2,1)S(1)}, bf16[2,128,128]{2,1,0:T(8,128)(2,1)S(1)}, u32[]{:S(2)}, u32[]{:S(2)}) %collective-permute-start) | collective-permute-done | bytes 65568 | tf_op jit(solution)/shard_map/while/body/eval_jaxpr/ppermute | solution.py:17
  206.1 7.3 %collective-permute-done = bf16[2,128,128]{2,1,0:T(8,128)(2,1)S(1)} collective-permute-done((bf16[2,128,128]{2,1,0:T(8,128)(2,1)S(1)}, bf16[2,128,128]{2,1,0:T(8,128)(2,1)S(1)}, u32[]{:S(2)}, u32[]{:S(2)}) %collective-permute-start) | collective-permute-done | bytes 65568 | tf_op jit(solution)/shard_map/while/body/eval_jaxpr/ppermute | solution.py:17
  215.0 7.3 %collective-permute-done = bf16[2,128,128]{2,1,0:T(8,128)(2,1)S(1)} collective-permute-done((bf16[2,128,128]{2,1,0:T(8,128)(2,1)S(1)}, bf16[2,128,128]{2,1,0:T(8,128)(2,1)S(1)}, u32[]{:S(2)}, u32[]{:S(2)}) %collective-permute-start) | collective-permute-done | bytes 65568 | tf_op jit(solution)/shard_map/while/body/eval_jaxpr/ppermute | solution.py:17
  222.9 0.7 fusion.57
  224.0 7.3 %collective-permute-done = bf16[2,128,128]{2,1,0:T(8,128)(2,1)S(1)} collective-permute-done((bf16[2,128,128]{2,1,0:T(8,128)(2,1)S(1)}, bf16[2,128,128]{2,1,0:T(8,128)(2,1)S(1)}, u32[]{:S(2)}, u32[]{:S(2)}) %collective-permute-start) | collective-permute-done | bytes 65568 | tf_op jit(solution)/shard_map/while/body/eval_jaxpr/ppermute | solution.py:17
  231.9 0.7 fusion.57
  232.9 7.3 %collective-permute-done = bf16[2,128,128]{2,1,0:T(8,128)(2,1)S(1)} collective-permute-done((bf16[2,128,128]{2,1,0:T(8,128)(2,1)S(1)}, bf16[2,128,128]{2,1,0:T(8,128)(2,1)S(1)}, u32[]{:S(2)}, u32[]{:S(2)}) %collective-permute-start) | collective-permute-done | bytes 65568 | tf_op jit(solution)/shard_map/while/body/eval_jaxpr/ppermute | solution.py:17
  241.8 7.3 %collective-permute-done = bf16[2,128,128]{2,1,0:T(8,128)(2,1)S(1)} collective-permute-done((bf16[2,128,128]{2,1,0:T(8,128)(2,1)S(1)}, bf16[2,128,128]{2,1,0:T(8,128)(2,1)S(1)}, u32[]{:S(2)}, u32[]{:S(2)}) %collective-permute-start) | collective-permute-done | bytes 65568 | tf_op jit(solution)/shard_map/while/body/eval_jaxpr/ppermute | solution.py:17
  250.7 7.3 %collective-permute-done = bf16[2,128,128]{2,1,0:T(8,128)(2,1)S(1)} collective-permute-done((bf16[2,128,128]{2,1,0:T(8,128)(2,1)S(1)}, bf16[2,128,128]{2,1,0:T(8,128)(2,1)S(1)}, u32[]{:S(2)}, u32[]{:S(2)}) %collective-permute-start) | collective-permute-done | bytes 65568 | tf_op jit(solution)/shard_map/while/body/eval_jaxpr/ppermute | solution.py:17
  258.6 0.7 fusion.57
  259.7 7.3 %collective-permute-done = bf16[2,128,128]{2,1,0:T(8,128)(2,1)S(1)} collective-permute-done((bf16[2,128,128]{2,1,0:T(8,128)(2,1)S(1)}, bf16[2,128,128]{2,1,0:T(8,128)(2,1)S(1)}, u32[]{:S(2)}, u32[]{:S(2)}) %collective-permute-start) | collective-permute-done | bytes 65568 | tf_op jit(solution)/shard_map/while/body/eval_jaxpr/ppermute | solution.py:17
  267.6 0.7 fusion.57
  268.6 7.3 %collective-permute-done = bf16[2,128,128]{2,1,0:T(8,128)(2,1)S(1)} collective-permute-done((bf16[2,128,128]{2,1,0:T(8,128)(2,1)S(1)}, bf16[2,128,128]{2,1,0:T(8,128)(2,1)S(1)}, u32[]{:S(2)}, u32[]{:S(2)}) %collective-permute-start) | collective-permute-done | bytes 65568 | tf_op jit(solution)/shard_map/while/body/eval_jaxpr/ppermute | solution.py:17
  276.5 0.7 fusion.57
  277.5 7.3 %collective-permute-done = bf16[2,128,128]{2,1,0:T(8,128)(2,1)S(1)} collective-permute-done((bf16[2,128,128]{2,1,0:T(8,128)(2,1)S(1)}, bf16[2,128,128]{2,1,0:T(8,128)(2,1)S(1)}, u32[]{:S(2)}, u32[]{:S(2)}) %collective-permute-start) | collective-permute-done | bytes 65568 | tf_op jit(solution)/shard_map/while/body/eval_jaxpr/ppermute | solution.py:17
  286.4 7.3 %collective-permute-done = bf16[2,128,128]{2,1,0:T(8,128)(2,1)S(1)} collective-permute-done((bf16[2,128,128]{2,1,0:T(8,128)(2,1)S(1)}, bf16[2,128,128]{2,1,0:T(8,128)(2,1)S(1)}, u32[]{:S(2)}, u32[]{:S(2)}) %collective-permute-start) | collective-permute-done | bytes 65568 | tf_op jit(solution)/shard_map/while/body/eval_jaxpr/ppermute | solution.py:17
  295.5 2.3 collective-permute-start.1
  297.8 8.4 %collective-permute-done.1 = bf16[128,2048]{0,1:T(8,128)(2,1)S(1)} collective-permute-done((bf16[128,2048]{0,1:T(8,128)(2,1)S(1)}, bf16[128,2048]{0,1:T(8,128)(2,1)S(1)}, u32[]{:S(2)}, u32[]{:S(2)}) %collective-permute-start.1) | collective-permute-done | bytes 524320 | tf_op jit(solution)/shard_map/ppermute | solution.py:17
  306.6 5.8 %psum.7 = f32[128]{0:T(128)S(1)} all-reduce(f32[128]{0:T(128)S(1)} %fusion.25), channel_id=1, replica_groups=mesh['pp'=2,'cp'=32,'tp'=4] {'tp'}, use_global_device_ids=true, to_apply=%region_11.12 | all-reduce | flops 128 | bytes 1024 | tf_op jit(solution)/shard_map/psum | solution.py:89
  312.4 4.1 %fusion.22 = bf16[128,1024]{1,0:T(8,128)(2,1)} fusion(bf16[1,2048,1024]{2,1,0:T(8,128)(2,1)} %param.13, bf16[128,2048]{0,1:T(8,128)(2,1)S(1)} %collective-permute-done.1, f32[2048]{0:T(1024)S(1)} %bitcast.111, f32[128]{0:T(128)S(1)} %add_rsqrt_fusion), kind=kOutput, calls=%fused_computation.41 | convolution fusion | flops 538050560 | bytes 4989440 | tf_op jit(solution)/shard_map/dot_general | solution.py:95
  316.7 70.1 %pmax.7 = f32[1,16]{1,0:T(1,128)} all-reduce(f32[1,16]{1,0:T(1,128)S(1)} %bitcast.112), channel_id=1, replica_groups=mesh['pp'=2,'cp'=32,'tp'=4] {'cp'}, use_global_device_ids=true, to_apply=%region_9.10 | all-reduce | flops 16 | bytes 128 | tf_op jit(solution)/shard_map/pmax | solution.py:86
  (373 shorter events, 34.2 us)
Async XLA Ops:
  7.2 6.3 %copy-start.2 = (s32[64]{0:T(128)S(1)}, s32[64]{0:T(128)}, u32[]{:S(2)}) copy-start(s32[64]{0:T(128)} %param.11) | copy-start | bytes 772
  7.2 5.5 %copy-start = (bf16[1,128,128]{2,1,0:T(8,128)(2,1)S(1)}, bf16[1,128,128]{2,1,0:T(8,128)(2,1)}, u32[]{:S(2)}) copy-start(bf16[1,128,128]{2,1,0:T(8,128)(2,1)} %param.10) | copy-start | bytes 98308
  7.2 379.6 %reduce-scatter.2.cloned.1.call-start = ((), (), s32[]{:S(2)}) async-start(), calls=%async_computation.1 | async-start | bytes 327680 | tf_op jit(solution)/shard_map/reduce_scatter | solution.py:96
  13.5 284.3 %copy-start.1 = (bf16[1,2048]{1,0:T(2,128)(2,1)S(1)}, bf16[1,2048]{1,0:T(2,128)(2,1)}, u32[]{:S(2)}) copy-start(bf16[1,2048]{1,0:T(2,128)(2,1)} %param.12) | copy-start | bytes 12292
  13.5 10.4 %collective-permute-start = (bf16[2,128,128]{2,1,0:T(8,128)(2,1)S(1)}, bf16[2,128,128]{2,1,0:T(8,128)(2,1)S(1)}, u32[]{:S(2)}, u32[]{:S(2)}) collective-permute-start(bf16[2,128,128]{2,1,0:T(8,128)(2,1)S(1)} %get-tuple-element.433), channel_id=1, source_target_pairs={{124,0},{0,4},{4,8},{8,12},{12,16},{16,20},{20,24},{24,28},{28,32}... | collective-permute-start | bytes 196616 | tf_op jit(solution)/shard_map/while/body/eval_jaxpr/ppermute | solution.py:17
  25.2 7.7 %collective-permute-start = (bf16[2,128,128]{2,1,0:T(8,128)(2,1)S(1)}, bf16[2,128,128]{2,1,0:T(8,128)(2,1)S(1)}, u32[]{:S(2)}, u32[]{:S(2)}) collective-permute-start(bf16[2,128,128]{2,1,0:T(8,128)(2,1)S(1)} %get-tuple-element.433), channel_id=1, source_target_pairs={{124,0},{0,4},{4,8},{8,12},{12,16},{16,20},{20,24},{24,28},{28,32}... | collective-permute-start | bytes 196616 | tf_op jit(solution)/shard_map/while/body/eval_jaxpr/ppermute | solution.py:17
  34.1 7.7 %collective-permute-start = (bf16[2,128,128]{2,1,0:T(8,128)(2,1)S(1)}, bf16[2,128,128]{2,1,0:T(8,128)(2,1)S(1)}, u32[]{:S(2)}, u32[]{:S(2)}) collective-permute-start(bf16[2,128,128]{2,1,0:T(8,128)(2,1)S(1)} %get-tuple-element.433), channel_id=1, source_target_pairs={{124,0},{0,4},{4,8},{8,12},{12,16},{16,20},{20,24},{24,28},{28,32}... | collective-permute-start | bytes 196616 | tf_op jit(solution)/shard_map/while/body/eval_jaxpr/ppermute | solution.py:17
  43.0 7.7 %collective-permute-start = (bf16[2,128,128]{2,1,0:T(8,128)(2,1)S(1)}, bf16[2,128,128]{2,1,0:T(8,128)(2,1)S(1)}, u32[]{:S(2)}, u32[]{:S(2)}) collective-permute-start(bf16[2,128,128]{2,1,0:T(8,128)(2,1)S(1)} %get-tuple-element.433), channel_id=1, source_target_pairs={{124,0},{0,4},{4,8},{8,12},{12,16},{16,20},{20,24},{24,28},{28,32}... | collective-permute-start | bytes 196616 | tf_op jit(solution)/shard_map/while/body/eval_jaxpr/ppermute | solution.py:17
  51.9 7.7 %collective-permute-start = (bf16[2,128,128]{2,1,0:T(8,128)(2,1)S(1)}, bf16[2,128,128]{2,1,0:T(8,128)(2,1)S(1)}, u32[]{:S(2)}, u32[]{:S(2)}) collective-permute-start(bf16[2,128,128]{2,1,0:T(8,128)(2,1)S(1)} %get-tuple-element.433), channel_id=1, source_target_pairs={{124,0},{0,4},{4,8},{8,12},{12,16},{16,20},{20,24},{24,28},{28,32}... | collective-permute-start | bytes 196616 | tf_op jit(solution)/shard_map/while/body/eval_jaxpr/ppermute | solution.py:17
  60.9 7.7 %collective-permute-start = (bf16[2,128,128]{2,1,0:T(8,128)(2,1)S(1)}, bf16[2,128,128]{2,1,0:T(8,128)(2,1)S(1)}, u32[]{:S(2)}, u32[]{:S(2)}) collective-permute-start(bf16[2,128,128]{2,1,0:T(8,128)(2,1)S(1)} %get-tuple-element.433), channel_id=1, source_target_pairs={{124,0},{0,4},{4,8},{8,12},{12,16},{16,20},{20,24},{24,28},{28,32}... | collective-permute-start | bytes 196616 | tf_op jit(solution)/shard_map/while/body/eval_jaxpr/ppermute | solution.py:17
  69.8 8.3 %collective-permute-start = (bf16[2,128,128]{2,1,0:T(8,128)(2,1)S(1)}, bf16[2,128,128]{2,1,0:T(8,128)(2,1)S(1)}, u32[]{:S(2)}, u32[]{:S(2)}) collective-permute-start(bf16[2,128,128]{2,1,0:T(8,128)(2,1)S(1)} %get-tuple-element.433), channel_id=1, source_target_pairs={{124,0},{0,4},{4,8},{8,12},{12,16},{16,20},{20,24},{24,28},{28,32}... | collective-permute-start | bytes 196616 | tf_op jit(solution)/shard_map/while/body/eval_jaxpr/ppermute | solution.py:17
  79.4 7.7 %collective-permute-start = (bf16[2,128,128]{2,1,0:T(8,128)(2,1)S(1)}, bf16[2,128,128]{2,1,0:T(8,128)(2,1)S(1)}, u32[]{:S(2)}, u32[]{:S(2)}) collective-permute-start(bf16[2,128,128]{2,1,0:T(8,128)(2,1)S(1)} %get-tuple-element.433), channel_id=1, source_target_pairs={{124,0},{0,4},{4,8},{8,12},{12,16},{16,20},{20,24},{24,28},{28,32}... | collective-permute-start | bytes 196616 | tf_op jit(solution)/shard_map/while/body/eval_jaxpr/ppermute | solution.py:17
  88.3 7.7 %collective-permute-start = (bf16[2,128,128]{2,1,0:T(8,128)(2,1)S(1)}, bf16[2,128,128]{2,1,0:T(8,128)(2,1)S(1)}, u32[]{:S(2)}, u32[]{:S(2)}) collective-permute-start(bf16[2,128,128]{2,1,0:T(8,128)(2,1)S(1)} %get-tuple-element.433), channel_id=1, source_target_pairs={{124,0},{0,4},{4,8},{8,12},{12,16},{16,20},{20,24},{24,28},{28,32}... | collective-permute-start | bytes 196616 | tf_op jit(solution)/shard_map/while/body/eval_jaxpr/ppermute | solution.py:17
  97.3 7.7 %collective-permute-start = (bf16[2,128,128]{2,1,0:T(8,128)(2,1)S(1)}, bf16[2,128,128]{2,1,0:T(8,128)(2,1)S(1)}, u32[]{:S(2)}, u32[]{:S(2)}) collective-permute-start(bf16[2,128,128]{2,1,0:T(8,128)(2,1)S(1)} %get-tuple-element.433), channel_id=1, source_target_pairs={{124,0},{0,4},{4,8},{8,12},{12,16},{16,20},{20,24},{24,28},{28,32}... | collective-permute-start | bytes 196616 | tf_op jit(solution)/shard_map/while/body/eval_jaxpr/ppermute | solution.py:17
  106.2 7.7 %collective-permute-start = (bf16[2,128,128]{2,1,0:T(8,128)(2,1)S(1)}, bf16[2,128,128]{2,1,0:T(8,128)(2,1)S(1)}, u32[]{:S(2)}, u32[]{:S(2)}) collective-permute-start(bf16[2,128,128]{2,1,0:T(8,128)(2,1)S(1)} %get-tuple-element.433), channel_id=1, source_target_pairs={{124,0},{0,4},{4,8},{8,12},{12,16},{16,20},{20,24},{24,28},{28,32}... | collective-permute-start | bytes 196616 | tf_op jit(solution)/shard_map/while/body/eval_jaxpr/ppermute | solution.py:17
  115.1 7.7 %collective-permute-start = (bf16[2,128,128]{2,1,0:T(8,128)(2,1)S(1)}, bf16[2,128,128]{2,1,0:T(8,128)(2,1)S(1)}, u32[]{:S(2)}, u32[]{:S(2)}) collective-permute-start(bf16[2,128,128]{2,1,0:T(8,128)(2,1)S(1)} %get-tuple-element.433), channel_id=1, source_target_pairs={{124,0},{0,4},{4,8},{8,12},{12,16},{16,20},{20,24},{24,28},{28,32}... | collective-permute-start | bytes 196616 | tf_op jit(solution)/shard_map/while/body/eval_jaxpr/ppermute | solution.py:17
  124.0 7.7 %collective-permute-start = (bf16[2,128,128]{2,1,0:T(8,128)(2,1)S(1)}, bf16[2,128,128]{2,1,0:T(8,128)(2,1)S(1)}, u32[]{:S(2)}, u32[]{:S(2)}) collective-permute-start(bf16[2,128,128]{2,1,0:T(8,128)(2,1)S(1)} %get-tuple-element.433), channel_id=1, source_target_pairs={{124,0},{0,4},{4,8},{8,12},{12,16},{16,20},{20,24},{24,28},{28,32}... | collective-permute-start | bytes 196616 | tf_op jit(solution)/shard_map/while/body/eval_jaxpr/ppermute | solution.py:17
  133.0 8.4 %collective-permute-start = (bf16[2,128,128]{2,1,0:T(8,128)(2,1)S(1)}, bf16[2,128,128]{2,1,0:T(8,128)(2,1)S(1)}, u32[]{:S(2)}, u32[]{:S(2)}) collective-permute-start(bf16[2,128,128]{2,1,0:T(8,128)(2,1)S(1)} %get-tuple-element.433), channel_id=1, source_target_pairs={{124,0},{0,4},{4,8},{8,12},{12,16},{16,20},{20,24},{24,28},{28,32}... | collective-permute-start | bytes 196616 | tf_op jit(solution)/shard_map/while/body/eval_jaxpr/ppermute | solution.py:17
  142.6 7.7 %collective-permute-start = (bf16[2,128,128]{2,1,0:T(8,128)(2,1)S(1)}, bf16[2,128,128]{2,1,0:T(8,128)(2,1)S(1)}, u32[]{:S(2)}, u32[]{:S(2)}) collective-permute-start(bf16[2,128,128]{2,1,0:T(8,128)(2,1)S(1)} %get-tuple-element.433), channel_id=1, source_target_pairs={{124,0},{0,4},{4,8},{8,12},{12,16},{16,20},{20,24},{24,28},{28,32}... | collective-permute-start | bytes 196616 | tf_op jit(solution)/shard_map/while/body/eval_jaxpr/ppermute | solution.py:17
  151.5 7.7 %collective-permute-start = (bf16[2,128,128]{2,1,0:T(8,128)(2,1)S(1)}, bf16[2,128,128]{2,1,0:T(8,128)(2,1)S(1)}, u32[]{:S(2)}, u32[]{:S(2)}) collective-permute-start(bf16[2,128,128]{2,1,0:T(8,128)(2,1)S(1)} %get-tuple-element.433), channel_id=1, source_target_pairs={{124,0},{0,4},{4,8},{8,12},{12,16},{16,20},{20,24},{24,28},{28,32}... | collective-permute-start | bytes 196616 | tf_op jit(solution)/shard_map/while/body/eval_jaxpr/ppermute | solution.py:17
  160.4 7.7 %collective-permute-start = (bf16[2,128,128]{2,1,0:T(8,128)(2,1)S(1)}, bf16[2,128,128]{2,1,0:T(8,128)(2,1)S(1)}, u32[]{:S(2)}, u32[]{:S(2)}) collective-permute-start(bf16[2,128,128]{2,1,0:T(8,128)(2,1)S(1)} %get-tuple-element.433), channel_id=1, source_target_pairs={{124,0},{0,4},{4,8},{8,12},{12,16},{16,20},{20,24},{24,28},{28,32}... | collective-permute-start | bytes 196616 | tf_op jit(solution)/shard_map/while/body/eval_jaxpr/ppermute | solution.py:17
  169.4 7.7 %collective-permute-start = (bf16[2,128,128]{2,1,0:T(8,128)(2,1)S(1)}, bf16[2,128,128]{2,1,0:T(8,128)(2,1)S(1)}, u32[]{:S(2)}, u32[]{:S(2)}) collective-permute-start(bf16[2,128,128]{2,1,0:T(8,128)(2,1)S(1)} %get-tuple-element.433), channel_id=1, source_target_pairs={{124,0},{0,4},{4,8},{8,12},{12,16},{16,20},{20,24},{24,28},{28,32}... | collective-permute-start | bytes 196616 | tf_op jit(solution)/shard_map/while/body/eval_jaxpr/ppermute | solution.py:17
  178.3 7.7 %collective-permute-start = (bf16[2,128,128]{2,1,0:T(8,128)(2,1)S(1)}, bf16[2,128,128]{2,1,0:T(8,128)(2,1)S(1)}, u32[]{:S(2)}, u32[]{:S(2)}) collective-permute-start(bf16[2,128,128]{2,1,0:T(8,128)(2,1)S(1)} %get-tuple-element.433), channel_id=1, source_target_pairs={{124,0},{0,4},{4,8},{8,12},{12,16},{16,20},{20,24},{24,28},{28,32}... | collective-permute-start | bytes 196616 | tf_op jit(solution)/shard_map/while/body/eval_jaxpr/ppermute | solution.py:17
  187.2 7.7 %collective-permute-start = (bf16[2,128,128]{2,1,0:T(8,128)(2,1)S(1)}, bf16[2,128,128]{2,1,0:T(8,128)(2,1)S(1)}, u32[]{:S(2)}, u32[]{:S(2)}) collective-permute-start(bf16[2,128,128]{2,1,0:T(8,128)(2,1)S(1)} %get-tuple-element.433), channel_id=1, source_target_pairs={{124,0},{0,4},{4,8},{8,12},{12,16},{16,20},{20,24},{24,28},{28,32}... | collective-permute-start | bytes 196616 | tf_op jit(solution)/shard_map/while/body/eval_jaxpr/ppermute | solution.py:17
  196.1 8.4 %collective-permute-start = (bf16[2,128,128]{2,1,0:T(8,128)(2,1)S(1)}, bf16[2,128,128]{2,1,0:T(8,128)(2,1)S(1)}, u32[]{:S(2)}, u32[]{:S(2)}) collective-permute-start(bf16[2,128,128]{2,1,0:T(8,128)(2,1)S(1)} %get-tuple-element.433), channel_id=1, source_target_pairs={{124,0},{0,4},{4,8},{8,12},{12,16},{16,20},{20,24},{24,28},{28,32}... | collective-permute-start | bytes 196616 | tf_op jit(solution)/shard_map/while/body/eval_jaxpr/ppermute | solution.py:17
  205.8 7.7 %collective-permute-start = (bf16[2,128,128]{2,1,0:T(8,128)(2,1)S(1)}, bf16[2,128,128]{2,1,0:T(8,128)(2,1)S(1)}, u32[]{:S(2)}, u32[]{:S(2)}) collective-permute-start(bf16[2,128,128]{2,1,0:T(8,128)(2,1)S(1)} %get-tuple-element.433), channel_id=1, source_target_pairs={{124,0},{0,4},{4,8},{8,12},{12,16},{16,20},{20,24},{24,28},{28,32}... | collective-permute-start | bytes 196616 | tf_op jit(solution)/shard_map/while/body/eval_jaxpr/ppermute | solution.py:17
  214.7 7.7 %collective-permute-start = (bf16[2,128,128]{2,1,0:T(8,128)(2,1)S(1)}, bf16[2,128,128]{2,1,0:T(8,128)(2,1)S(1)}, u32[]{:S(2)}, u32[]{:S(2)}) collective-permute-start(bf16[2,128,128]{2,1,0:T(8,128)(2,1)S(1)} %get-tuple-element.433), channel_id=1, source_target_pairs={{124,0},{0,4},{4,8},{8,12},{12,16},{16,20},{20,24},{24,28},{28,32}... | collective-permute-start | bytes 196616 | tf_op jit(solution)/shard_map/while/body/eval_jaxpr/ppermute | solution.py:17
  223.6 7.7 %collective-permute-start = (bf16[2,128,128]{2,1,0:T(8,128)(2,1)S(1)}, bf16[2,128,128]{2,1,0:T(8,128)(2,1)S(1)}, u32[]{:S(2)}, u32[]{:S(2)}) collective-permute-start(bf16[2,128,128]{2,1,0:T(8,128)(2,1)S(1)} %get-tuple-element.433), channel_id=1, source_target_pairs={{124,0},{0,4},{4,8},{8,12},{12,16},{16,20},{20,24},{24,28},{28,32}... | collective-permute-start | bytes 196616 | tf_op jit(solution)/shard_map/while/body/eval_jaxpr/ppermute | solution.py:17
  232.5 7.7 %collective-permute-start = (bf16[2,128,128]{2,1,0:T(8,128)(2,1)S(1)}, bf16[2,128,128]{2,1,0:T(8,128)(2,1)S(1)}, u32[]{:S(2)}, u32[]{:S(2)}) collective-permute-start(bf16[2,128,128]{2,1,0:T(8,128)(2,1)S(1)} %get-tuple-element.433), channel_id=1, source_target_pairs={{124,0},{0,4},{4,8},{8,12},{12,16},{16,20},{20,24},{24,28},{28,32}... | collective-permute-start | bytes 196616 | tf_op jit(solution)/shard_map/while/body/eval_jaxpr/ppermute | solution.py:17
  241.5 7.7 %collective-permute-start = (bf16[2,128,128]{2,1,0:T(8,128)(2,1)S(1)}, bf16[2,128,128]{2,1,0:T(8,128)(2,1)S(1)}, u32[]{:S(2)}, u32[]{:S(2)}) collective-permute-start(bf16[2,128,128]{2,1,0:T(8,128)(2,1)S(1)} %get-tuple-element.433), channel_id=1, source_target_pairs={{124,0},{0,4},{4,8},{8,12},{12,16},{16,20},{20,24},{24,28},{28,32}... | collective-permute-start | bytes 196616 | tf_op jit(solution)/shard_map/while/body/eval_jaxpr/ppermute | solution.py:17
  250.4 7.7 %collective-permute-start = (bf16[2,128,128]{2,1,0:T(8,128)(2,1)S(1)}, bf16[2,128,128]{2,1,0:T(8,128)(2,1)S(1)}, u32[]{:S(2)}, u32[]{:S(2)}) collective-permute-start(bf16[2,128,128]{2,1,0:T(8,128)(2,1)S(1)} %get-tuple-element.433), channel_id=1, source_target_pairs={{124,0},{0,4},{4,8},{8,12},{12,16},{16,20},{20,24},{24,28},{28,32}... | collective-permute-start | bytes 196616 | tf_op jit(solution)/shard_map/while/body/eval_jaxpr/ppermute | solution.py:17
  259.3 7.7 %collective-permute-start = (bf16[2,128,128]{2,1,0:T(8,128)(2,1)S(1)}, bf16[2,128,128]{2,1,0:T(8,128)(2,1)S(1)}, u32[]{:S(2)}, u32[]{:S(2)}) collective-permute-start(bf16[2,128,128]{2,1,0:T(8,128)(2,1)S(1)} %get-tuple-element.433), channel_id=1, source_target_pairs={{124,0},{0,4},{4,8},{8,12},{12,16},{16,20},{20,24},{24,28},{28,32}... | collective-permute-start | bytes 196616 | tf_op jit(solution)/shard_map/while/body/eval_jaxpr/ppermute | solution.py:17
  268.3 7.7 %collective-permute-start = (bf16[2,128,128]{2,1,0:T(8,128)(2,1)S(1)}, bf16[2,128,128]{2,1,0:T(8,128)(2,1)S(1)}, u32[]{:S(2)}, u32[]{:S(2)}) collective-permute-start(bf16[2,128,128]{2,1,0:T(8,128)(2,1)S(1)} %get-tuple-element.433), channel_id=1, source_target_pairs={{124,0},{0,4},{4,8},{8,12},{12,16},{16,20},{20,24},{24,28},{28,32}... | collective-permute-start | bytes 196616 | tf_op jit(solution)/shard_map/while/body/eval_jaxpr/ppermute | solution.py:17
  277.2 7.7 %collective-permute-start = (bf16[2,128,128]{2,1,0:T(8,128)(2,1)S(1)}, bf16[2,128,128]{2,1,0:T(8,128)(2,1)S(1)}, u32[]{:S(2)}, u32[]{:S(2)}) collective-permute-start(bf16[2,128,128]{2,1,0:T(8,128)(2,1)S(1)} %get-tuple-element.433), channel_id=1, source_target_pairs={{124,0},{0,4},{4,8},{8,12},{12,16},{16,20},{20,24},{24,28},{28,32}... | collective-permute-start | bytes 196616 | tf_op jit(solution)/shard_map/while/body/eval_jaxpr/ppermute | solution.py:17
  286.1 7.7 %collective-permute-start = (bf16[2,128,128]{2,1,0:T(8,128)(2,1)S(1)}, bf16[2,128,128]{2,1,0:T(8,128)(2,1)S(1)}, u32[]{:S(2)}, u32[]{:S(2)}) collective-permute-start(bf16[2,128,128]{2,1,0:T(8,128)(2,1)S(1)} %get-tuple-element.433), channel_id=1, source_target_pairs={{124,0},{0,4},{4,8},{8,12},{12,16},{16,20},{20,24},{24,28},{28,32}... | collective-permute-start | bytes 196616 | tf_op jit(solution)/shard_map/while/body/eval_jaxpr/ppermute | solution.py:17
  295.5 10.8 %collective-permute-start.1 = (bf16[128,2048]{0,1:T(8,128)(2,1)S(1)}, bf16[128,2048]{0,1:T(8,128)(2,1)S(1)}, u32[]{:S(2)}, u32[]{:S(2)}) collective-permute-start(bf16[128,2048]{0,1:T(8,128)(2,1)S(1)} %bitcast.109), channel_id=1, source_target_pairs={{128,0},{0,128},{129,1},{1,129},{130,2},{2,130},{131,3},{3,131},{1... | collective-permute-start | bytes 1572872 | tf_op jit(solution)/shard_map/ppermute | solution.py:17
Sparse Core Ops, SparseCore 0:
  316.7 12.0 reduce-scatter.1
where the time goes:
time: 394 us
  waiting for transfers between devices  239 us (61%)
  blocking collectives  76 us (19%)
  matrix products  35.9 us (9%)
  other arithmetic  15.5 us (4%)
  between operations  14.2 us (4%)
  starting transfers between devices  6.87 us (2%)
    ppermute x32, waiting for transfers between devices, shifted(): return lax.ppermute(block, axis, route)  239 us
    pmax x1, blocking collectives, on_device(): max_logits = lax.pmax(local_peak, 'cp')  70.1 us
    dot_general x32, matrix products, attend(): jnp.einsum('tkgs,skd->tkgd', weights.astype(jnp.bfloat16), v_part, prefer...  21 us
    dot_general x32, matrix products, attend(): jnp.einsum('tkgd,skd->tkgs', query_block, k_part, preferred_element_type=...  10.7 us
  transfers between devices with their start and end apart: 33, of which 32 were waited for; matrix products, arithmetic and copies ran while one was open for 2% of the time, Pallas kernels for 0%

commit v1 on v0

v1 whole, which is shorter than its diff:
```python
import math

import jax
import jax.numpy as jnp
from jax import lax
from jax.experimental import pallas as pl
from jax.experimental.pallas import tpu as pltpu
from jax.sharding import PartitionSpec as P

BF = jnp.bfloat16
F32 = jnp.float32
MESH = pl.DeviceIdType.MESH

DH = 128
ROWS = 128
HALF = 64
HEADS = 16
NX, NZ = 4, 8
SLOTS = NX * NZ
FEATURES = 8192
GROUP = 4
TQ = GROUP * ROWS
TK = 1024
VROWS = 144
COLS = 1024
OUT = 256
BIG = 2.0**100
SCALE = 1.0 / math.sqrt(DH)
EXP2 = SCALE * math.log2(math.e)
N_SEM = 128


def device(y, x, z, c):
    return ((y % 4) // 2, (x % NX) * NZ + z % NZ, (y % 2) * 2 + c)


class Traffic:
    def __init__(self, send, recv):
        self.send, self.recv = send, recv
        self.copies = {}
        self.after = {}
        self.need = {}
        self.order = []

    def add(self, name, src, dst, to, after=()):
        i = len(self.copies)
        self.copies[name] = pltpu.make_async_remote_copy(
            src_ref=src,
            dst_ref=dst,
            send_sem=self.send.at[i],
            recv_sem=self.recv.at[i],
            device_id=to,
            device_id_type=MESH,
        )
        self.need[name] = set(after)
        for a in after:
            self.after.setdefault(a, []).append(name)

    def start(self, name):
        self.copies[name].start()

    def arrive(self, name):
        self.copies[name].wait_recv()
        for child in self.after.get(name, ()):
            self.need[child].discard(name)
            if not self.need[child]:
                self.start(child)

    def sent(self):
        for c in self.copies.values():
            c.wait_send()


def kernel(
    order, q_hbm, k_hbm, v_ref, gain_ref, w_hbm,
    kv_out, max_out,
    kbuf, vt, vown, qs, w, s_buf, acc_out, parts, got, sqbuf, sqgot, mxbuf, mxgot, mx2, mxgot2,
    send, recv, local,
):
    pp, cp, tp = lax.axis_index("pp"), lax.axis_index("cp"), lax.axis_index("tp")
    y, x, z, c = pp * 2 + tp // 2, cp // NZ, cp % NZ, tp % 2

    wcopy = pltpu.make_async_copy(w_hbm, w, local.at[0])
    wcopy.start()

    barrier = pltpu.get_barrier_semaphore()
    peers = [device(y, x + d, z, c) for d in (1, 2, 3)]
    peers += [device(y, x, z + d, c) for d in (1, 2, 6, 7)]
    peers += [device(y + 2, x, z + d, c) for d in range(NZ)]
    mates = [device(y, x, z, 1 - c), device(y // 2 * 2 + 1 - y % 2, x, z, c)]
    mates += [device(y // 2 * 2 + 1 - y % 2, x, z, 1 - c)]
    for d in peers + mates:
        pl.semaphore_signal(barrier, inc=1, device_id=d, device_id_type=MESH)

    vown[...] = v_ref[...].astype(F32).T.astype(BF)

    t = Traffic(send, recv)

    def ks(dz, dx, lo=0, n=ROWS):
        return kbuf.at[pl.ds(((dz % NZ) * NX + dx % NX) * ROWS + lo, n), pl.ds(0, DH)]

    def vs(dz, dx, lo=0, n=DH):
        return vt.at[(dz % NZ) * NX + dx % NX, pl.ds(lo, n), :]

    partner = device(y + 2, x, z, c)
    t.add("k", k_hbm, ks(0, 0), partner)
    t.add("v", vown, vs(0, 0), partner)
    for h in range(HEADS):
        t.add(
            ("q", h),
            q_hbm.at[:, pl.ds(h * DH, DH)],
            qs.at[pl.ds(h * ROWS, ROWS), pl.ds(0, DH)],
            partner,
        )
    for d in (1, 3, 2):
        t.add(("kx", d), ks(0, 0), ks(0, -d), device(y, x + d, z, c), ["k"])
    for s in range(4):
        for dx in (0, 1, 3, 2):
            first = ["k"] if dx == 0 else [("kx", 4 - dx)]
            n, lo = (ROWS, 0) if s < 3 else (HALF, HALF)
            t.add(
                ("ku", s, dx), ks(-s, dx, 0, n), ks(-s - 1, dx, 0, n),
                device(y, x, z + 1, c), first if s == 0 else [("ku", s - 1, dx)],
            )
            t.add(
                ("kd", s, dx), ks(s, dx, lo, n), ks(s + 1, dx, lo, n),
                device(y, x, z - 1, c), first if s == 0 else [("kd", s - 1, dx)],
            )
    for d in (1, -1, 2, -2):
        t.add(("vz", d), vs(0, 0), vs(-d, 0), device(y, x, z + d, c), ["v"])
    for d in (1, -1):
        lo = 0 if d > 0 else HALF
        t.add(("vz", 3 * d), vs(-2 * d, 0), vs(-3 * d, 0), device(y, x, z + d, c), [("vz", 2 * d)])
        t.add(
            ("vz", 4 * d), vs(-2 * d, 0, lo, HALF), vs(-4 * d, 0, lo, HALF),
            device(y, x, z + 2 * d, c), [("vz", 2 * d)],
        )
    for dz in (0, 1, -1, 2, -2, 3, -3, 4):
        came = ["v"] if dz == 0 else [("vz", 4), ("vz", -4)] if dz == 4 else [("vz", -dz)]
        for d in (1, 3, 2):
            t.add(("vx", dz, d), vs(dz, 0), vs(dz, -d), device(y, x + d, z, c), came)

    pl.semaphore_wait(barrier, len(peers) + len(mates))

    for name in ["k", "v"] + [("q", h) for h in range(HEADS)]:
        t.start(name)

    row = lax.broadcasted_iota(jnp.int32, (ROWS, DH), 0)
    lane = lax.broadcasted_iota(jnp.int32, (ROWS, DH), 1)
    mine = (lane >= HALF) == (row >= HALF)
    off = lane % HALF
    q_mask = jnp.where(mine & ((off == 0) | (off > row % HALF)), -BIG, 0.0).astype(BF)
    for h in range(HEADS):
        qs[pl.ds(h * ROWS, ROWS), pl.ds(DH, DH)] = q_mask
    hrow = lax.broadcasted_iota(jnp.int32, (HALF, DH), 0)
    hlane = lax.broadcasted_iota(jnp.int32, (HALF, DH), 1)
    hoff = hlane % HALF
    after_all = (hoff == 0).astype(F32)
    in_block = ((hoff == hrow) & (hoff > 0)).astype(F32)
    half_id = jnp.where(hlane < HALF, order[2 * cp], order[2 * cp + 1])
    for slot in range(SLOTS):
        dz, dx = slot // NX, slot % NX
        src = ((x + dx) % NX) * NZ + (z + dz) % NZ
        for b in range(2):
            block = order[2 * src + b]
            k_mask = jnp.where(half_id < block, after_all, jnp.where(half_id == block, in_block, 0.0))
            kbuf[pl.ds(slot * ROWS + b * HALF, HALF), pl.ds(DH, DH)] = k_mask.astype(BF)
        vt[slot, pl.ds(DH, VROWS - DH), :] = jnp.ones((VROWS - DH, ROWS), BF)

    t.arrive("k")
    t.arrive("v")
    for d in (1, 3, 2):
        t.arrive(("kx", d))
    for d in (1, -1, 2, -2):
        t.arrive(("vz", d))
    for s in range(4):
        for dx in (0, 1, 3, 2):
            t.arrive(("ku", s, dx))
            t.arrive(("kd", s, dx))
        if s == 0:
            for d in (3, -3, 4, -4):
                t.arrive(("vz", d))
    for dz in (0, 1, -1, 2, -2, 3, -3, 4):
        for d in (1, 3, 2):
            t.arrive(("vx", dz, d))
    for h in range(HEADS):
        t.arrive(("q", h))
    wcopy.wait()

    steps = SLOTS * ROWS // TK
    per = TK // ROWS

    def score(first, j, slot):
        s = lax.dot_general(
            kbuf[pl.ds(j * TK, TK), :], qs[pl.ds(first, TQ), :],
            (((1,), (1,)), ((), ())), preferred_element_type=F32,
        )
        s_buf[slot] = s
        return jnp.max(s, axis=0, keepdims=True)

    acc_out[...] = jnp.zeros_like(acc_out)
    sqbuf[...] = jnp.zeros_like(sqbuf)
    mxbuf[...] = jnp.full_like(mxbuf, -BIG)
    groups = HEADS // GROUP
    mlane = lax.broadcasted_iota(jnp.int32, (8, DH), 1)

    def group(g, peak):
        first = pl.multiple_of(g * TQ, TQ)
        following = pl.multiple_of(jnp.minimum(g + 1, groups - 1) * TQ, TQ)
        top = total = None
        for j in range(steps):
            new_top = peak if j == 0 else jnp.maximum(top, peak)
            p = jnp.exp2((s_buf[j % 2] - new_top) * EXP2).astype(BF)
            if j < steps - 1:
                peak = score(first, j + 1, (j + 1) % 2)
            else:
                peak = score(following, 0, (j + 1) % 2)
            values = jnp.concatenate([vt[j * per + i] for i in range(per)], axis=1)
            part = jnp.dot(values, p, preferred_element_type=F32)
            total = part if j == 0 else total * jnp.exp2((top - new_top) * EXP2) + part
            top = new_top
        attn = (total[:DH, :] / total[DH : DH + 1, :]).astype(BF).astype(F32)
        square = jnp.sum(attn * attn, axis=0, keepdims=True)
        pieces = []
        for i in range(GROUP):
            cut = slice(i * ROWS, (i + 1) * ROWS)
            sqbuf[...] += jnp.broadcast_to(square[:, cut], (8, ROWS))
            best = jnp.max(top[:, cut], axis=1, keepdims=True) * SCALE
            mxbuf[...] = jnp.where(mlane == g * GROUP + i, best, mxbuf[...])
            gain = gain_ref[pl.ds(g * GROUP + i, 1), :]
            pieces.append((attn[:, cut].T * gain).astype(BF))
        acc_out[...] += jnp.dot(
            jnp.concatenate(pieces, axis=1), w[pl.ds(first, TQ), :], preferred_element_type=F32
        )
        return peak

    lax.fori_loop(0, groups, group, score(0, 0, 0))

    for d in (1, 2, 3):
        t.add(("mx", d), mxbuf, mxgot.at[d], device(y, x + d, z, c))
        t.start(("mx", d))
    for j in range(4):
        parts[j] = acc_out[:, pl.ds(j * OUT, OUT)].astype(BF)
    for i, to in reversed(list(enumerate(mates))):
        t.add(("sq", i), sqbuf, sqgot.at[i], to)
        t.add(("rs", i), parts.at[to[2]], got.at[i], to)
        t.start(("sq", i))
        t.start(("rs", i))
    for d in (1, 2, 3):
        t.arrive(("mx", d))
    mx2[...] = jnp.maximum(jnp.maximum(mxbuf[...], mxgot[1]), jnp.maximum(mxgot[2], mxgot[3]))
    for d in range(NZ):
        t.add(("mz", d), mx2, mxgot2.at[d], device(y + 2, x, z + d, c))
        t.start(("mz", d))
    for i in range(3):
        t.arrive(("sq", i))
        t.arrive(("rs", i))
    square = sqbuf[...] + sqgot[0] + sqgot[1] + sqgot[2]
    inverse = lax.rsqrt(square * (1.0 / FEATURES) + 1e-05)
    inverse = jnp.broadcast_to(inverse[:1, :], (ROWS, ROWS)).T
    own = parts[tp].astype(F32)
    result = own + got[0].astype(F32) + got[1].astype(F32) + got[2].astype(F32)
    kv_out[...] = (result * jnp.concatenate([inverse, inverse], axis=1)).astype(BF)
    for d in range(NZ):
        t.arrive(("mz", d))
    best = mxgot2[0]
    for d in range(1, NZ):
        best = jnp.maximum(best, mxgot2[d])
    max_out[...] = best
    t.sent()


def on_device(queries, key_vectors, value_vectors, block_order, norm_gain, kv_weight):
    any_ = pl.BlockSpec(memory_space=pl.ANY)
    vmem = pl.BlockSpec(memory_space=pltpu.VMEM)
    kv, peak = pl.pallas_call(
        kernel,
        out_shape=(jax.ShapeDtypeStruct((ROWS, OUT), BF), jax.ShapeDtypeStruct((8, DH), F32)),
        in_specs=[pl.BlockSpec(memory_space=pltpu.SMEM), any_, any_, vmem, vmem, any_],
        out_specs=(vmem, vmem),
        scratch_shapes=[
            pltpu.VMEM((SLOTS * ROWS, 2 * DH), BF),
            pltpu.VMEM((SLOTS, VROWS, ROWS), BF),
            pltpu.VMEM((DH, ROWS), BF),
            pltpu.VMEM((HEADS * ROWS, 2 * DH), BF),
            pltpu.VMEM((HEADS * DH, COLS), BF),
            pltpu.VMEM((2, TK, TQ), F32),
            pltpu.VMEM((ROWS, COLS), F32),
            pltpu.VMEM((4, ROWS, OUT), BF),
            pltpu.VMEM((3, ROWS, OUT), BF),
            pltpu.VMEM((8, DH), F32),
            pltpu.VMEM((3, 8, DH), F32),
            pltpu.VMEM((8, DH), F32),
            pltpu.VMEM((4, 8, DH), F32),
            pltpu.VMEM((8, DH), F32),
            pltpu.VMEM((NZ, 8, DH), F32),
            pltpu.SemaphoreType.DMA((N_SEM,)),
            pltpu.SemaphoreType.DMA((N_SEM,)),
            pltpu.SemaphoreType.DMA((1,)),
        ],
        compiler_params=pltpu.CompilerParams(
            collective_id=0, has_side_effects=True, vmem_limit_bytes=48 << 20
        ),
        name="attention",
    )(
        block_order,
        queries[0],
        key_vectors[0],
        value_vectors[0],
        norm_gain[0].astype(F32).reshape(HEADS, DH),
        kv_weight[0],
    )
    return peak[:1, :HEADS], kv[None]


def solution(mesh):
    return jax.shard_map(
        on_device,
        mesh=mesh,
        in_specs=(
            P("pp", "cp", "tp"),
            P("pp", "cp", "tp"),
            P("pp", "cp", "tp"),
            P(),
            P("pp", "tp"),
            P("pp", "tp", None),
        ),
        out_specs=(P("pp", "tp"), P("pp", "cp", "tp")),
        check_vma=False,
    )
```

time: 394 us -> 65.2 us (0.17)
  waiting for transfers between devices: 239 us -> 0 us
  blocking collectives: 76 us -> 0 us
  Pallas kernels: 0 us -> 56.8 us
  matrix products: 35.9 us -> 0 us
  other arithmetic: 15.5 us -> 0.71 us
  between operations: 14.2 us -> 0.65 us
  starting transfers between devices: 6.87 us -> 0 us
    ppermute x32 -> x0, waiting for transfers between devices: 239 us -> none  [shifted(): return lax.ppermute(block, axis, route)]
    pmax x1 -> x0, blocking collectives: 70.1 us -> none  [on_device(): max_logits = lax.pmax(local_peak, 'cp')]
    pallas_call x0 -> x1, Pallas kernels: none -> 56.8 us  [on_device(): pl.pallas_call(kernel, out_shape=(jax.ShapeDtypeStruct((ROWS, OUT), BF),...]
    dot_general x65 -> x0, matrix products: 35.9 us -> none  [the longest x32 21 us: attend(): jnp.einsum('tkgs,skd->tkgd', weights.astype(jnp.bfloat16), v_part, prefer...]
    reduce_sum x65 -> x0, other arithmetic: 10.2 us -> none  [the longest x32 6.28 us: attend(): running_sum = running_sum * shrink + jnp.sum(weights, axis=3)]
    ppermute x32 -> x0, starting transfers between devices: 6.83 us -> none  [shifted(): return lax.ppermute(block, axis, route)]
    psum x1 -> x0, blocking collectives: 5.83 us -> none  [on_device(): squares = lax.psum(jnp.sum(wide * wide, axis=1), 'tp')]
  transfers between devices with their start and end apart: 33 -> 0, of which waited for: 32 -> 0; matrix products, arithmetic and copies ran while one was open for 2% -> 0% of each run, Pallas kernels for 0% -> 0%
where the time goes in v1:
time: 65.2 us; the launch traced here: 64.7 us
  Pallas kernels  56.8 us (87%)
  local copies, waits for them, and re-layouts  6.54 us (10%)
  other arithmetic  0.71 us (1%)
    pallas_call x1, Pallas kernels, on_device(): pl.pallas_call(kernel, out_shape=(jax.ShapeDtypeStruct((ROWS, OUT), BF),...  56.8 us
    unnamed x11, local copies, waits for them, and re-layouts  6.02 us

profile of v1, /device:TPU:8, one launch (start us, length us, event | category | flops | bytes accessed | tf_op | source)
XLA Modules:
  0.0 64.7 jit_solution(2782103898165506403)
XLA Ops:
  0.6 0.7 %convert_element_type.9 = f32[1,2048]{1,0:T(1,128)S(1)} convert(bf16[1,2048]{1,0:T(2,128)(2,1)} %param.10) | non-fusion elementwise | flops 2048 | bytes 12288 | tf_op jit(solution)/shard_map/convert_element_type | solution.py:310
  1.3 0.0 copy-start
  1.4 2.2 %copy-done = bf16[1,2048,1024]{2,1,0:T(8,128)(2,1)S(1)} copy-done((bf16[1,2048,1024]{2,1,0:T(8,128)(2,1)S(1)}, bf16[1,2048,1024]{2,1,0:T(8,128)(2,1)}, u32[]{:S(2)}) %copy-start) | copy-done | bytes 4194328
  3.5 0.0 copy-start.1
  3.5 1.0 %copy-done.1 = bf16[1,128,2048]{2,1,0:T(8,128)(2,1)S(1)} copy-done((bf16[1,128,2048]{2,1,0:T(8,128)(2,1)S(1)}, bf16[1,128,2048]{2,1,0:T(8,128)(2,1)}, u32[]{:S(2)}) %copy-start.1) | copy-done | bytes 524312
  4.6 0.0 copy-start.2
  4.6 0.8 %copy-done.2 = bf16[1,128,128]{2,1,0:T(8,128)(2,1)S(1)} copy-done((bf16[1,128,128]{2,1,0:T(8,128)(2,1)S(1)}, bf16[1,128,128]{2,1,0:T(8,128)(2,1)}, u32[]{:S(2)}) %copy-start.2) | copy-done | bytes 32792
  5.3 0.0 copy-start.3
  5.3 0.8 %copy-done.3 = bf16[1,128,128]{2,1,0:T(8,128)(2,1)S(1)} copy-done((bf16[1,128,128]{2,1,0:T(8,128)(2,1)S(1)}, bf16[1,128,128]{2,1,0:T(8,128)(2,1)}, u32[]{:S(2)}) %copy-start.3) | copy-done | bytes 32792
  6.1 0.0 copy-start.4
  6.1 0.7 %copy-done.4 = s32[64]{0:T(128)S(1)} copy-done((s32[64]{0:T(128)S(1)}, s32[64]{0:T(128)}, u32[]{:S(2)}) %copy-start.4) | copy-done | bytes 280
  6.7 56.8 %attention.1 = (bf16[128,256]{1,0:T(8,128)(2,1)S(1)}, f32[8,128]{1,0:T(8,128)S(1)}) custom-call(s32[64]{0:T(128)S(1)} %copy-done.4, bf16[128,2048]{1,0:T(8,128)(2,1)S(1)} %bitcast.7, bf16[128,128]{1,0:T(8,128)(2,1)S(1)} %bitcast.9, bf16[128,128]{1,0:T(8,128)(2,1)S(1)} %bitcast.10, f32[16,128]{1,0:T(8,128)S(1)} %bitcast.11, bf16[2048,1024]{1,0:T(8,128)(2,1)S(1)} %bitcast.6), custom_call_target="tpu_custom_call" | custom-call | tf_op jit(solution)/shard_map/attention/pallas_call | solution.py:276
  63.6 0.5 slice.3
  64.1 0.6 copy.9
Async XLA Ops:
  1.3 2.2 %copy-start = (bf16[1,2048,1024]{2,1,0:T(8,128)(2,1)S(1)}, bf16[1,2048,1024]{2,1,0:T(8,128)(2,1)}, u32[]{:S(2)}) copy-start(bf16[1,2048,1024]{2,1,0:T(8,128)(2,1)} %param.11) | copy-start | bytes 12582916
  3.5 1.0 %copy-start.1 = (bf16[1,128,2048]{2,1,0:T(8,128)(2,1)S(1)}, bf16[1,128,2048]{2,1,0:T(8,128)(2,1)}, u32[]{:S(2)}) copy-start(bf16[1,128,2048]{2,1,0:T(8,128)(2,1)} %param.6) | copy-start | bytes 1572868
  4.6 0.8 %copy-start.2 = (bf16[1,128,128]{2,1,0:T(8,128)(2,1)S(1)}, bf16[1,128,128]{2,1,0:T(8,128)(2,1)}, u32[]{:S(2)}) copy-start(bf16[1,128,128]{2,1,0:T(8,128)(2,1)} %param.7) | copy-start | bytes 98308
  5.3 0.8 %copy-start.3 = (bf16[1,128,128]{2,1,0:T(8,128)(2,1)S(1)}, bf16[1,128,128]{2,1,0:T(8,128)(2,1)}, u32[]{:S(2)}) copy-start(bf16[1,128,128]{2,1,0:T(8,128)(2,1)} %param.8) | copy-start | bytes 98308
  6.1 0.7 %copy-start.4 = (s32[64]{0:T(128)S(1)}, s32[64]{0:T(128)}, u32[]{:S(2)}) copy-start(s32[64]{0:T(128)} %order.1) | copy-start | bytes 772

commit v2 on v1

v2 whole, which is shorter than its diff:
```python
import math

import jax
import jax.numpy as jnp
from jax import lax
from jax.experimental import pallas as pl
from jax.experimental.pallas import tpu as pltpu
from jax.sharding import PartitionSpec as P

BF = jnp.bfloat16
F32 = jnp.float32
MESH = pl.DeviceIdType.MESH

DH = 128
ROWS = 128
HALF = 64
HEADS = 16
NX, NZ = 4, 8
SLOTS = NX * NZ
FEATURES = 8192
GROUP = 4
TQ = GROUP * ROWS
TK = 6 * ROWS
VROWS = 144
COLS = 1024
OUT = 256
BIG = 2.0**100
SCALE = 1.0 / math.sqrt(DH)
EXP2 = SCALE * math.log2(math.e)
N_SEM = 128
VMEM_LIMIT = 57 << 20
TILES = (
    [(0, dx) for dx in range(NX)],
    [(1, 0), (-1, 0), (2, 0), (-2, 0)],
    [(dz, dx) for dx in (1, 3, 2) for dz in (1, -1)],
    [(dz, dx) for dx in (1, 3, 2) for dz in (2, -2)],
    [(dz, dx) for dx in (0, 1, 3, 2) for dz in (3, -3)],
    [(4, dx) for dx in range(NX)],
)
SLOT = {(dz % NZ, dx): i for i, (dz, dx) in enumerate(sum(TILES, []))}
FIRST = [SLOT[t[0][0] % NZ, t[0][1]] for t in TILES]
SIZE = [len(t) for t in TILES]
LATE = 4


def ring(i, *dxs):
    return ("arrive", *[(a, i, dx) for dx in dxs for a in ("ku", "kd")])


SCHEDULE = (
    [("arrive", ("kx", 3), ("kx", 1), ("kx", 2))]
    + [("arrive", ("vz", 2), ("vz", -2), ("vz", 1), ("vz", -1)), ring(0, 0)]
    + [(0, 0), ("flush",), ("arrive", ("vz", 3), ("vz", -3), ("vz", 4), ("vz", -4))]
    + [ring(0, 1, 3, 2), ring(1, 0)]
    + [(1, 0), (0, 1), (1, 1), (2, 0), (2, 1), (0, 2), ring(1, 1, 3), (1, 2), ring(1, 2)]
    + [(2, 2), ring(2, 0), (3, 0), (3, 1), (3, 2), (0, 3), ring(2, 1, 3), (1, 3), ring(2, 2)]
    + [(2, 3), (3, 3)]
)


def slot_of(dz, dx):
    return SLOT[dz % NZ, dx % NX]


def device(y, x, z, c):
    return ((y % 4) // 2, (x % NX) * NZ + z % NZ, (y % 2) * 2 + c)


class Traffic:
    def __init__(self, send, recv):
        self.send, self.recv = send, recv
        self.copies = {}
        self.after = {}
        self.need = {}
        self.came = set()
        self.started = []

    def add(self, name, src, dst, to, after=()):
        i = len(self.copies)
        self.copies[name] = pltpu.make_async_remote_copy(
            src_ref=src,
            dst_ref=dst,
            send_sem=self.send.at[i],
            recv_sem=self.recv.at[i],
            device_id=to,
            device_id_type=MESH,
        )
        self.need[name] = set(after)
        for a in after:
            self.after.setdefault(a, []).append(name)

    def start(self, name):
        self.copies[name].start()
        self.started.append(name)

    def arrive(self, *names):
        for name in names:
            if name in self.came:
                continue
            self.came.add(name)
            self.copies[name].wait_recv()
            for child in self.after.get(name, ()):
                self.need[child].discard(name)
                if not self.need[child]:
                    self.start(child)

    def sent(self):
        for name in self.started:
            self.copies[name].wait_send()
        self.started = []


def kernel(
    order, gain_ref, q_hbm, k_hbm, v_hbm, w_hbm,
    kv_out, max_out,
    kbuf, vt, vin, vown, qs, w, s_buf, s_late, tops, totals, acc_out, parts, got,
    sqbuf, sqgot, mxbuf, mxgot, mx2, mxgot2, send, recv, local,
):
    pp, cp, tp = lax.axis_index("pp"), lax.axis_index("cp"), lax.axis_index("tp")
    y, x, z, c = pp * 2 + tp // 2, cp // NZ, cp % NZ, tp % 2

    vcopy = pltpu.make_async_copy(v_hbm, vin, local.at[1])
    vcopy.start()
    barrier = pltpu.get_barrier_semaphore()
    peers = [device(y, x + d, z, c) for d in (1, 2, 3)]
    peers += [device(y, x, z + d, c) for d in (1, 2, 6, 7)]
    peers += [device(y + 2, x, z + d, c) for d in range(NZ)]
    other = y // 2 * 2 + 1 - y % 2
    mates = [device(y, x, z, 1 - c), device(other, x, z, c), device(other, x, z, 1 - c)]
    for d in peers + mates:
        pl.semaphore_signal(barrier, inc=1, device_id=d, device_id_type=MESH)
    wcopy = pltpu.make_async_copy(w_hbm, w, local.at[0])
    wcopy.start()

    vcopy.wait()
    vown[...] = vin[...].astype(F32).T.astype(BF)

    t = Traffic(send, recv)

    def ks(dz, dx, lo=0, n=ROWS):
        return kbuf.at[pl.ds(slot_of(dz, dx) * ROWS + lo, n), pl.ds(0, DH)]

    def vs(dz, dx, lo=0, n=DH):
        return vt.at[slot_of(dz, dx), pl.ds(lo, n), :]

    partner = device(y + 2, x, z, c)
    t.add("k", k_hbm, ks(0, 0), partner)
    t.add("v", vown, vs(0, 0), partner)
    for h in range(HEADS):
        t.add(
            ("q", h),
            q_hbm.at[:, pl.ds(h * DH, DH)],
            qs.at[pl.ds(h * ROWS, ROWS), pl.ds(0, DH)],
            partner,
        )
    for d in (1, -1, 2, -2):
        t.add(("vz", d), vs(0, 0), vs(-d, 0), device(y, x, z + d, c), ["v"])
    for d in (1, 3, 2):
        t.add(("kx", d), ks(0, 0), ks(0, -d), device(y, x + d, z, c), ["k"])
    for d in (1, -1):
        lo = 0 if d > 0 else HALF
        far, near = device(y, x, z + 2 * d, c), device(y, x, z + d, c)
        t.add(("vz", 3 * d), vs(-2 * d, 0), vs(-3 * d, 0), near, [("vz", 2 * d)])
        t.add(("vz", 4 * d), vs(-2 * d, 0, lo, HALF), vs(4, 0, lo, HALF), far, [("vz", 2 * d)])
    for i in range(4):
        for dx in (0, 1, 3, 2):
            first = ["k"] if dx == 0 else [("kx", 4 - dx)]
            n, lo = (ROWS, 0) if i < 3 else (HALF, HALF)
            t.add(
                ("ku", i, dx), ks(-i, dx, 0, n), ks(-i - 1, dx, 0, n),
                device(y, x, z + 1, c), first if i == 0 else [("ku", i - 1, dx)],
            )
            t.add(
                ("kd", i, dx), ks(i, dx, lo, n), ks(i + 1, dx, lo, n),
                device(y, x, z - 1, c), first if i == 0 else [("kd", i - 1, dx)],
            )
    for dz in (0, 1, -1, 2, -2, 3, -3, 4):
        came = ["v"] if dz == 0 else [("vz", 4), ("vz", -4)] if dz == 4 else [("vz", -dz)]
        for d in (1, 3, 2):
            t.add(("vx", dz, d), vs(dz, 0), vs(dz, -d), device(y, x + d, z, c), came)

    pl.semaphore_wait(barrier, len(peers) + len(mates))

    for name in ["k", "v"] + [("q", h) for h in range(HEADS)]:
        t.start(name)

    row = lax.broadcasted_iota(jnp.int32, (ROWS, DH), 0)
    lane = lax.broadcasted_iota(jnp.int32, (ROWS, DH), 1)
    mine = (lane >= HALF) == (row >= HALF)
    off = lane % HALF
    q_mask = jnp.where(mine & ((off == 0) | (off > row % HALF)), -BIG, 0.0).astype(BF)
    for h in range(HEADS):
        qs[pl.ds(h * ROWS, ROWS), pl.ds(DH, DH)] = q_mask
    hrow = lax.broadcasted_iota(jnp.int32, (HALF, DH), 0)
    hlane = lax.broadcasted_iota(jnp.int32, (HALF, DH), 1)
    hoff = hlane % HALF
    after_all = (hoff == 0).astype(F32)
    in_block = ((hoff == hrow) & (hoff > 0)).astype(F32)
    half_id = jnp.where(hlane < HALF, order[2 * cp], order[2 * cp + 1])

    def masks(dz):
        for dx in range(NX):
            slot = slot_of(dz, dx)
            src = ((x + dx) % NX) * NZ + (z + dz) % NZ
            for b in range(2):
                block = order[2 * src + b]
                k_mask = jnp.where(half_id < block, after_all, jnp.where(half_id == block, in_block, 0.0))
                kbuf[pl.ds(slot * ROWS + b * HALF, HALF), pl.ds(DH, DH)] = k_mask.astype(BF)
            vt[slot, pl.ds(DH, VROWS - DH), :] = jnp.ones((VROWS - DH, ROWS), BF)

    for dz in range(NZ):
        masks(dz)
    acc_out[...] = jnp.zeros_like(acc_out)
    sqbuf[...] = jnp.zeros_like(sqbuf)
    mxbuf[...] = jnp.full_like(mxbuf, -BIG)
    mlane = lax.broadcasted_iota(jnp.int32, (8, DH), 1)
    t.arrive("k", "v")

    def score(g, tile, into):
        first, size = FIRST[tile] * ROWS, SIZE[tile] * ROWS
        s = lax.dot_general(
            kbuf[pl.ds(first, size), :], qs[pl.ds(g * TQ, TQ), :],
            (((1,), (1,)), ((), ())), preferred_element_type=F32,
        )
        into[...] = s
        return jnp.max(s, axis=0, keepdims=True)

    def ready(g, tile):
        t.arrive(*[("q", h) for h in range(g * GROUP, (g + 1) * GROUP)])
        for dz, dx in TILES[tile]:
            if dz == 0:
                t.arrive("k" if dx == 0 else ("kx", 4 - dx))
            elif dz == 4:
                t.arrive(("ku", 3, dx), ("kd", 3, dx))
            else:
                t.arrive(("kd" if dz > 0 else "ku", abs(dz) - 1, dx))

    def ready_v(tile):
        for dz, dx in TILES[tile]:
            t.arrive(*(["v"] if dz == 0 else [("vz", 4), ("vz", -4)] if dz == 4 else [("vz", -dz)]))
            if dx:
                t.arrive(("vx", dz, 4 - dx))

    def weigh(g, first, size, scores, top, ahead=()):
        p = jnp.exp2((scores[...] - top) * EXP2).astype(BF)
        peaks = [score(*a) for a in ahead]
        values = jnp.concatenate([vt[first + i] for i in range(size)], axis=1)
        part = jnp.dot(values, p, preferred_element_type=F32)
        if g in seen:
            totals[g] = totals[g] * jnp.exp2((tops[g] - top) * EXP2) + part
        else:
            totals[g] = part
        tops[g] = top
        seen.add(g)
        return peaks

    def finish(g):
        total = totals[g]
        attn = (total[:DH, :] / total[DH : DH + 1, :]).astype(BF).astype(F32)
        square = jnp.sum(attn * attn, axis=0, keepdims=True)
        pieces = []
        for i in range(GROUP):
            cut = slice(i * ROWS, (i + 1) * ROWS)
            sqbuf[...] += jnp.broadcast_to(square[:, cut], (8, ROWS))
            gain = gain_ref[:, pl.ds((g * GROUP + i) * DH, DH)].astype(F32)
            pieces.append((attn[:, cut].T * gain).astype(BF))
        acc_out[...] += jnp.dot(
            jnp.concatenate(pieces, axis=1), w[pl.ds(g * TQ, TQ), :], preferred_element_type=F32
        )

    def largest(g, top):
        for i in range(GROUP):
            best = jnp.max(top[:, i * ROWS : (i + 1) * ROWS], axis=1, keepdims=True) * SCALE
            mxbuf[...] = jnp.where(mlane == g * GROUP + i, best, mxbuf[...])

    def buffer(n, tile):
        return s_buf.at[n % 2, pl.ds(0, SIZE[tile] * ROWS), :]

    def late(g, tile):
        return s_late.at[g, pl.ds((FIRST[tile] - FIRST[LATE]) * ROWS, SIZE[tile] * ROWS), :]

    groups = HEADS // GROUP
    steps = [i for i in SCHEDULE if isinstance(i[0], int)]
    seen = set()
    n = 0
    peak = None
    for k, item in enumerate(SCHEDULE):
        if item[0] == "arrive":
            t.arrive(*item[1:])
        if not isinstance(item[0], int):
            continue
        g, tile = item
        if peak is None:
            ready(g, tile)
            peak = score(g, tile, buffer(n, tile))
        ready_v(tile)
        ahead = []
        if n + 1 == len(steps):
            ready(0, LATE)
            ahead = [(0, LATE, late(0, LATE))]
        elif SCHEDULE[k + 1][0] != "flush":
            ready(*steps[n + 1])
            ahead = [(*steps[n + 1], buffer(n + 1, steps[n + 1][1]))]
        top = jnp.maximum(tops[g], peak) if g in seen else peak
        peaks = weigh(g, FIRST[tile], SIZE[tile], buffer(n, tile), top, ahead)
        peak = peaks[0] if peaks else None
        n += 1
    late_tops = [peak] + [score(g, LATE, late(g, LATE)) for g in range(1, groups)]
    t.sent()
    for g in range(groups):
        ready(g, LATE + 1)
        late_top = score(g, LATE + 1, late(g, LATE + 1))
        late_tops[g] = jnp.maximum(jnp.maximum(tops[g], late_tops[g]), late_top)
        largest(g, late_tops[g])
    for d in (1, 2, 3):
        t.add(("mx", d), mxbuf, mxgot.at[d], device(y, x + d, z, c))
        t.start(("mx", d))
    ready_v(LATE)
    ready_v(LATE + 1)
    wcopy.wait()
    for g in range(groups):
        weigh(g, FIRST[LATE], SLOTS - FIRST[LATE], s_late.at[g], late_tops[g])
        finish(g)
        if g == 2:
            t.arrive(*[("mx", d) for d in (1, 2, 3)])
            mx2[...] = jnp.maximum(jnp.maximum(mxbuf[...], mxgot[1]), jnp.maximum(mxgot[2], mxgot[3]))
            for d in range(NZ):
                t.add(("mz", d), mx2, mxgot2.at[d], device(y + 2, x, z + d, c))
                t.start(("mz", d))

    for j in range(4):
        parts[j] = acc_out[:, pl.ds(j * OUT, OUT)].astype(BF)
    for i, to in reversed(list(enumerate(mates))):
        t.add(("sq", i), sqbuf, sqgot.at[i], to)
        t.add(("rs", i), parts.at[to[2]], got.at[i], to)
        t.start(("sq", i))
        t.start(("rs", i))
    t.arrive(*[(a, i) for i in range(3) for a in ("sq", "rs")])
    square = sqbuf[...] + sqgot[0] + sqgot[1] + sqgot[2]
    inverse = lax.rsqrt(square * (1.0 / FEATURES) + 1e-05)
    inverse = jnp.broadcast_to(inverse[:1, :], (ROWS, ROWS)).T
    own = parts[tp].astype(F32)
    result = own + got[0].astype(F32) + got[1].astype(F32) + got[2].astype(F32)
    kv_out[...] = (result * jnp.concatenate([inverse, inverse], axis=1)).astype(BF)
    t.arrive(*[("mz", d) for d in range(NZ)])
    best = mxgot2[0]
    for d in range(1, NZ):
        best = jnp.maximum(best, mxgot2[d])
    max_out[...] = best[:1, :HEADS]
    t.sent()


def on_device(queries, key_vectors, value_vectors, block_order, norm_gain, kv_weight):
    any_ = pl.BlockSpec(memory_space=pl.ANY)
    vmem = pl.BlockSpec(memory_space=pltpu.VMEM)
    kv, peak = pl.pallas_call(
        kernel,
        out_shape=(jax.ShapeDtypeStruct((ROWS, OUT), BF), jax.ShapeDtypeStruct((1, HEADS), F32)),
        in_specs=[pl.BlockSpec(memory_space=pltpu.SMEM), vmem, any_, any_, any_, any_],
        out_specs=(vmem, vmem),
        scratch_shapes=[
            pltpu.VMEM((SLOTS * ROWS, 2 * DH), BF),
            pltpu.VMEM((SLOTS, VROWS, ROWS), BF),
            pltpu.VMEM((ROWS, DH), BF),
            pltpu.VMEM((DH, ROWS), BF),
            pltpu.VMEM((HEADS * ROWS, 2 * DH), BF),
            pltpu.VMEM((HEADS * DH, COLS), BF),
            pltpu.VMEM((2, TK, TQ), F32),
            pltpu.VMEM((HEADS // GROUP, (SLOTS - FIRST[LATE]) * ROWS, TQ), F32),
            pltpu.VMEM((HEADS // GROUP, 1, TQ), F32),
            pltpu.VMEM((HEADS // GROUP, VROWS, TQ), F32),
            pltpu.VMEM((ROWS, COLS), F32),
            pltpu.VMEM((4, ROWS, OUT), BF),
            pltpu.VMEM((3, ROWS, OUT), BF),
            pltpu.VMEM((8, DH), F32),
            pltpu.VMEM((3, 8, DH), F32),
            pltpu.VMEM((8, DH), F32),
            pltpu.VMEM((4, 8, DH), F32),
            pltpu.VMEM((8, DH), F32),
            pltpu.VMEM((NZ, 8, DH), F32),
            pltpu.SemaphoreType.DMA((N_SEM,)),
            pltpu.SemaphoreType.DMA((N_SEM,)),
            pltpu.SemaphoreType.DMA((2,)),
        ],
        compiler_params=pltpu.CompilerParams(
            collective_id=0, has_side_effects=True, vmem_limit_bytes=VMEM_LIMIT
        ),
        name="attention",
    )(
        block_order,
        norm_gain,
        queries[0],
        key_vectors[0],
        value_vectors[0],
        kv_weight[0],
    )
    return peak, kv[None]


def solution(mesh):
    return jax.shard_map(
        on_device,
        mesh=mesh,
        in_specs=(
            P("pp", "cp", "tp"),
            P("pp", "cp", "tp"),
            P("pp", "cp", "tp"),
            P(),
            P("pp", "tp"),
            P("pp", "tp", None),
        ),
        out_specs=(P("pp", "tp"), P("pp", "cp", "tp")),
        check_vma=False,
    )
```

time: 65.2 us -> 54.1 us (0.83)
  Pallas kernels: 56.8 us -> 50.7 us
  local copies, waits for them, and re-layouts: 6.54 us -> 2.59 us
  other arithmetic: 0.71 us -> 0 us
    pallas_call x1, Pallas kernels: 56.8 us -> 50.7 us  [on_device(): pl.pallas_call(kernel, out_shape=(jax.ShapeDtypeStruct((ROWS, OUT), BF),...]
    unnamed x11 -> x2, local copies, waits for them, and re-layouts: 6.02 us -> 2.59 us
    convert_element_type x1 -> x0, other arithmetic: 0.71 us -> none  [on_device(): norm_gain[0].astype(F32).reshape(HEADS, DH)]
where the time goes in v2:
time: 54.1 us; the launch traced here: 53.9 us
  Pallas kernels  50.7 us (94%)
  local copies, waits for them, and re-layouts  2.59 us (5%)
  between operations  0.64 us (1%)
    pallas_call x1, Pallas kernels, on_device(): pl.pallas_call(kernel, out_shape=(jax.ShapeDtypeStruct((ROWS, OUT), BF),...  50.7 us
    unnamed x2, local copies, waits for them, and re-layouts  2.59 us

profile of v2, /device:TPU:8, one launch (start us, length us, event | category | flops | bytes accessed | tf_op | source)
XLA Modules:
  0.0 53.9 jit_solution(16795930974372127850)
XLA Ops:
  0.6 50.7 %attention.1 = (bf16[128,256]{1,0:T(8,128)(2,1)}, f32[1,16]{1,0:T(1,128)}) custom-call(s32[64]{0:T(128)} %order.1, bf16[1,2048]{1,0:T(2,128)(2,1)} %gain_ref.1, bf16[128,2048]{1,0:T(8,128)(2,1)} %bitcast.6, bf16[128,128]{1,0:T(8,128)(2,1)} %bitcast.8, bf16[128,128]{1,0:T(8,128)(2,1)} %bitcast.9, bf16[2048,1024]{1,0:T(8,128)(2,1)} %bitcast.5), custom_call_target="tpu_custom_call" | custom-call | tf_op jit(solution)/shard_map/attention/pallas_call | solution.py:356
  51.3 1.1 %copy.10 = f32[1,16]{1,0:T(1,128)} copy(f32[1,16]{1,0:T(1,128)} %get-tuple-element.8) | data formatting | bytes 128
  52.4 1.5 %copy.11 = bf16[1,128,256]{2,1,0:T(8,128)(2,1)} copy(bf16[1,128,256]{2,1,0:T(8,128)(2,1)} %bitcast.7) | data formatting | bytes 131072

commit v3 on v2

--- a/solution.py
+++ b/solution.py
@@ -20,7 +20,7 @@
 FEATURES = 8192
 GROUP = 4
 TQ = GROUP * ROWS
-TK = 6 * ROWS
+TK = 8 * ROWS
 VROWS = 144
 COLS = 1024
 OUT = 256
@@ -28,7 +28,7 @@
 SCALE = 1.0 / math.sqrt(DH)
 EXP2 = SCALE * math.log2(math.e)
 N_SEM = 128
-VMEM_LIMIT = 57 << 20
+VMEM_LIMIT = 48 << 20
 TILES = (
     [(0, dx) for dx in range(NX)],
     [(1, 0), (-1, 0), (2, 0), (-2, 0)],
@@ -40,7 +40,7 @@
 SLOT = {(dz % NZ, dx): i for i, (dz, dx) in enumerate(sum(TILES, []))}
 FIRST = [SLOT[t[0][0] % NZ, t[0][1]] for t in TILES]
 SIZE = [len(t) for t in TILES]
-LATE = 4
+LATE = 5
 
 
 def ring(i, *dxs):
@@ -54,7 +54,7 @@
     + [ring(0, 1, 3, 2), ring(1, 0)]
     + [(1, 0), (0, 1), (1, 1), (2, 0), (2, 1), (0, 2), ring(1, 1, 3), (1, 2), ring(1, 2)]
     + [(2, 2), ring(2, 0), (3, 0), (3, 1), (3, 2), (0, 3), ring(2, 1, 3), (1, 3), ring(2, 2)]
-    + [(2, 3), (3, 3)]
+    + [(2, 3), (3, 3), (0, 4), (1, 4), (2, 4), (3, 4), ("flush",)]
 )
 
 
@@ -111,9 +111,9 @@
 
 
 def kernel(
-    order, gain_ref, q_hbm, k_hbm, v_hbm, w_hbm,
+    order_hbm, gain_hbm, q_hbm, k_hbm, v_hbm, w_hbm,
     kv_out, max_out,
-    kbuf, vt, vin, vown, qs, w, s_buf, s_late, tops, totals, acc_out, parts, got,
+    order, gain_ref, kbuf, vt, vin, vown, qs, w, s_buf, s_late, tops, totals, acc_out, parts, got,
     sqbuf, sqgot, mxbuf, mxgot, mx2, mxgot2, send, recv, local,
 ):
     pp, cp, tp = lax.axis_index("pp"), lax.axis_index("cp"), lax.axis_index("tp")
@@ -121,6 +121,10 @@
 
     vcopy = pltpu.make_async_copy(v_hbm, vin, local.at[1])
     vcopy.start()
+    ocopy = pltpu.make_async_copy(order_hbm, order, local.at[2])
+    ocopy.start()
+    gcopy = pltpu.make_async_copy(gain_hbm, gain_ref, local.at[3])
+    gcopy.start()
     barrier = pltpu.get_barrier_semaphore()
     peers = [device(y, x + d, z, c) for d in (1, 2, 3)]
     peers += [device(y, x, z + d, c) for d in (1, 2, 6, 7)]
@@ -133,6 +137,8 @@
     wcopy.start()
 
     vcopy.wait()
+    ocopy.wait()
+    gcopy.wait()
     vown[...] = vin[...].astype(F32).T.astype(BF)
 
     t = Traffic(send, recv)
@@ -276,9 +282,6 @@
     def buffer(n, tile):
         return s_buf.at[n % 2, pl.ds(0, SIZE[tile] * ROWS), :]
 
-    def late(g, tile):
-        return s_late.at[g, pl.ds((FIRST[tile] - FIRST[LATE]) * ROWS, SIZE[tile] * ROWS), :]
-
     groups = HEADS // GROUP
     steps = [i for i in SCHEDULE if isinstance(i[0], int)]
     seen = set()
@@ -295,31 +298,26 @@
             peak = score(g, tile, buffer(n, tile))
         ready_v(tile)
         ahead = []
-        if n + 1 == len(steps):
-            ready(0, LATE)
-            ahead = [(0, LATE, late(0, LATE))]
-        elif SCHEDULE[k + 1][0] != "flush":
+        if SCHEDULE[k + 1][0] != "flush":
             ready(*steps[n + 1])
             ahead = [(*steps[n + 1], buffer(n + 1, steps[n + 1][1]))]
         top = jnp.maximum(tops[g], peak) if g in seen else peak
         peaks = weigh(g, FIRST[tile], SIZE[tile], buffer(n, tile), top, ahead)
         peak = peaks[0] if peaks else None
         n += 1
-    late_tops = [peak] + [score(g, LATE, late(g, LATE)) for g in range(1, groups)]
     t.sent()
+    late_tops = []
     for g in range(groups):
-        ready(g, LATE + 1)
-        late_top = score(g, LATE + 1, late(g, LATE + 1))
-        late_tops[g] = jnp.maximum(jnp.maximum(tops[g], late_tops[g]), late_top)
+        ready(g, LATE)
+        late_tops.append(jnp.maximum(tops[g], score(g, LATE, s_late.at[g])))
         largest(g, late_tops[g])
     for d in (1, 2, 3):
         t.add(("mx", d), mxbuf, mxgot.at[d], device(y, x + d, z, c))
         t.start(("mx", d))
     ready_v(LATE)
-    ready_v(LATE + 1)
     wcopy.wait()
     for g in range(groups):
-        weigh(g, FIRST[LATE], SLOTS - FIRST[LATE], s_late.at[g], late_tops[g])
+        weigh(g, FIRST[LATE], SIZE[LATE], s_late.at[g], late_tops[g])
         finish(g)
         if g == 2:
             t.arrive(*[("mx", d) for d in (1, 2, 3)])
@@ -351,14 +349,16 @@
 
 
 def on_device(queries, key_vectors, value_vectors, block_order, norm_gain, kv_weight):
-    any_ = pl.BlockSpec(memory_space=pl.ANY)
+    hbm = pl.BlockSpec(memory_space=pltpu.HBM)
     vmem = pl.BlockSpec(memory_space=pltpu.VMEM)
     kv, peak = pl.pallas_call(
         kernel,
         out_shape=(jax.ShapeDtypeStruct((ROWS, OUT), BF), jax.ShapeDtypeStruct((1, HEADS), F32)),
-        in_specs=[pl.BlockSpec(memory_space=pltpu.SMEM), vmem, any_, any_, any_, any_],
+        in_specs=[hbm] * 6,
         out_specs=(vmem, vmem),
         scratch_shapes=[
+            pltpu.SMEM((2 * SLOTS,), jnp.int32),
+            pltpu.VMEM((1, HEADS * DH), BF),
             pltpu.VMEM((SLOTS * ROWS, 2 * DH), BF),
             pltpu.VMEM((SLOTS, VROWS, ROWS), BF),
             pltpu.VMEM((ROWS, DH), BF),
@@ -366,7 +366,7 @@
             pltpu.VMEM((HEADS * ROWS, 2 * DH), BF),
             pltpu.VMEM((HEADS * DH, COLS), BF),
             pltpu.VMEM((2, TK, TQ), F32),
-            pltpu.VMEM((HEADS // GROUP, (SLOTS - FIRST[LATE]) * ROWS, TQ), F32),
+            pltpu.VMEM((HEADS // GROUP, SIZE[LATE] * ROWS, TQ), F32),
             pltpu.VMEM((HEADS // GROUP, 1, TQ), F32),
             pltpu.VMEM((HEADS // GROUP, VROWS, TQ), F32),
             pltpu.VMEM((ROWS, COLS), F32),
@@ -380,19 +380,17 @@
             pltpu.VMEM((NZ, 8, DH), F32),
             pltpu.SemaphoreType.DMA((N_SEM,)),
             pltpu.SemaphoreType.DMA((N_SEM,)),
-            pltpu.SemaphoreType.DMA((2,)),
+            pltpu.SemaphoreType.DMA((4,)),
         ],
         compiler_params=pltpu.CompilerParams(
             collective_id=0, has_side_effects=True, vmem_limit_bytes=VMEM_LIMIT
         ),
         name="attention",
     )(
-        block_order,
-        norm_gain,
-        queries[0],
-        key_vectors[0],
-        value_vectors[0],
-        kv_weight[0],
+        *[
+            pltpu.with_memory_space_constraint(a, pltpu.HBM)
+            for a in (block_order, norm_gain, queries[0], key_vectors[0], value_vectors[0], kv_weight[0])
+        ]
     )
     return peak, kv[None]
 

time: 54.1 us -> 51.6 us (0.954)
  local copies, waits for them, and re-layouts: 2.59 us -> 1.14 us
  Pallas kernels: 50.7 us -> 49.7 us
    unnamed x2, local copies, waits for them, and re-layouts: 2.59 us -> 1.14 us
    pallas_call x1, Pallas kernels: 50.7 us -> 49.7 us  [on_device(): pl.pallas_call(kernel, out_shape=(jax.ShapeDtypeStruct((ROWS, OUT), BF),...]
where the time goes in v3:
time: 51.6 us; the launch traced here: 51.5 us
  Pallas kernels  49.7 us (96%)
  local copies, waits for them, and re-layouts  1.14 us (2%)
  between operations  0.64 us (1%)
    pallas_call x1, Pallas kernels, on_device(): pl.pallas_call(kernel, out_shape=(jax.ShapeDtypeStruct((ROWS, OUT), BF),...  49.7 us
    unnamed x2, local copies, waits for them, and re-layouts  1.14 us

profile of v3, /device:TPU:8, one launch (start us, length us, event | category | flops | bytes accessed | tf_op | source)
XLA Modules:
  0.0 51.5 jit_solution(8021298964914360686)
XLA Ops:
  0.6 49.7 %attention.1 = (bf16[128,256]{1,0:T(8,128)(2,1)S(1)}, f32[1,16]{1,0:T(1,128)S(1)}) custom-call(s32[64]{0:T(128)} %order_hbm.1, bf16[1,2048]{1,0:T(2,128)(2,1)} %gain_hbm.1, bf16[128,2048]{1,0:T(8,128)(2,1)} %bitcast.7, bf16[128,128]{1,0:T(8,128)(2,1)} %bitcast.8, bf16[128,128]{1,0:T(8,128)(2,1)} %bitcast.9, bf16[2048,1024]{1,0:T(8,128)(2,1)} %bitcast.6), custom_call_target="tpu_custom_call" | custom-call | tf_op jit(solution)/shard_map/attention/pallas_call | solution.py:354
  50.4 0.5 copy.10
  50.9 0.6 %copy.11 = bf16[1,128,256]{2,1,0:T(8,128)(2,1)} copy(bf16[1,128,256]{2,1,0:T(8,128)(2,1)S(1)} %bitcast.5) | data formatting | bytes 131072

commit v4 on v3

--- a/solution.py
+++ b/solution.py
@@ -33,9 +33,9 @@
     [(0, dx) for dx in range(NX)],
     [(1, 0), (-1, 0), (2, 0), (-2, 0)],
     [(dz, dx) for dx in (1, 3, 2) for dz in (1, -1)],
-    [(dz, dx) for dx in (1, 3, 2) for dz in (2, -2)],
-    [(dz, dx) for dx in (0, 1, 3, 2) for dz in (3, -3)],
-    [(4, dx) for dx in range(NX)],
+    [(dz, dx) for dx in (1, 3, 2) for dz in (2, -2)] + [(3, 0), (-3, 0)],
+    [(dz, dx) for dx in (1, 3, 2) for dz in (3, -3)] + [(4, 0)],
+    [(4, dx) for dx in (1, 3, 2)],
 )
 SLOT = {(dz % NZ, dx): i for i, (dz, dx) in enumerate(sum(TILES, []))}
 FIRST = [SLOT[t[0][0] % NZ, t[0][1]] for t in TILES]
@@ -49,11 +49,12 @@
 
 SCHEDULE = (
     [("arrive", ("kx", 3), ("kx", 1), ("kx", 2))]
-    + [("arrive", ("vz", 2), ("vz", -2), ("vz", 1), ("vz", -1)), ring(0, 0)]
-    + [(0, 0), ("flush",), ("arrive", ("vz", 3), ("vz", -3), ("vz", 4), ("vz", -4))]
-    + [ring(0, 1, 3, 2), ring(1, 0)]
-    + [(1, 0), (0, 1), (1, 1), (2, 0), (2, 1), (0, 2), ring(1, 1, 3), (1, 2), ring(1, 2)]
-    + [(2, 2), ring(2, 0), (3, 0), (3, 1), (3, 2), (0, 3), ring(2, 1, 3), (1, 3), ring(2, 2)]
+    + [("arrive", ("vz", 1), ("vz", -1)), ring(0, 0)]
+    + [(0, 0), ("flush",), ring(0, 1, 3, 2), ("arrive", ("vz", 2), ("vz", -2)), ring(1, 0)]
+    + [(1, 0), (0, 1), (1, 1), (2, 0), (2, 1), ("arrive", ("vz", 3), ("vz", -3))]
+    + [(0, 2), ring(1, 1, 3), (1, 2), ring(1, 2)]
+    + [(2, 2), ring(2, 0), (3, 0), (3, 1), ("arrive", ("vz", 4), ("vz", -4))]
+    + [(3, 2), (0, 3), ring(2, 1, 3), (1, 3), ring(2, 2)]
     + [(2, 3), (3, 3), (0, 4), (1, 4), (2, 4), (3, 4), ("flush",)]
 )
 
@@ -127,7 +128,7 @@
     gcopy.start()
     barrier = pltpu.get_barrier_semaphore()
     peers = [device(y, x + d, z, c) for d in (1, 2, 3)]
-    peers += [device(y, x, z + d, c) for d in (1, 2, 6, 7)]
+    peers += [device(y, x, z + d, c) for d in (1, 7)]
     peers += [device(y + 2, x, z + d, c) for d in range(NZ)]
     other = y // 2 * 2 + 1 - y % 2
     mates = [device(y, x, z, 1 - c), device(other, x, z, c), device(other, x, z, 1 - c)]
@@ -159,15 +160,14 @@
             qs.at[pl.ds(h * ROWS, ROWS), pl.ds(0, DH)],
             partner,
         )
-    for d in (1, -1, 2, -2):
-        t.add(("vz", d), vs(0, 0), vs(-d, 0), device(y, x, z + d, c), ["v"])
+    for d in (1, -1):
+        near = device(y, x, z + d, c)
+        for i in range(4):
+            n, lo = (DH, 0) if i < 3 else (HALF, 0 if d > 0 else HALF)
+            src, dst = vs(-i * d, 0, lo, n), vs(-(i + 1) * d, 0, lo, n)
+            t.add(("vz", (i + 1) * d), src, dst, near, [("vz", i * d)] if i else ["v"])
     for d in (1, 3, 2):
         t.add(("kx", d), ks(0, 0), ks(0, -d), device(y, x + d, z, c), ["k"])
-    for d in (1, -1):
-        lo = 0 if d > 0 else HALF
-        far, near = device(y, x, z + 2 * d, c), device(y, x, z + d, c)
-        t.add(("vz", 3 * d), vs(-2 * d, 0), vs(-3 * d, 0), near, [("vz", 2 * d)])
-        t.add(("vz", 4 * d), vs(-2 * d, 0, lo, HALF), vs(4, 0, lo, HALF), far, [("vz", 2 * d)])
     for i in range(4):
         for dx in (0, 1, 3, 2):
             first = ["k"] if dx == 0 else [("kx", 4 - dx)]
@@ -216,7 +216,6 @@
 
     for dz in range(NZ):
         masks(dz)
-    acc_out[...] = jnp.zeros_like(acc_out)
     sqbuf[...] = jnp.zeros_like(sqbuf)
     mxbuf[...] = jnp.full_like(mxbuf, -BIG)
     mlane = lax.broadcasted_iota(jnp.int32, (8, DH), 1)
@@ -262,7 +261,7 @@
 
     def finish(g):
         total = totals[g]
-        attn = (total[:DH, :] / total[DH : DH + 1, :]).astype(BF).astype(F32)
+        attn = (total[:DH, :] * (1.0 / total[DH : DH + 1, :])).astype(BF).astype(F32)
         square = jnp.sum(attn * attn, axis=0, keepdims=True)
         pieces = []
         for i in range(GROUP):
@@ -270,9 +269,17 @@
             sqbuf[...] += jnp.broadcast_to(square[:, cut], (8, ROWS))
             gain = gain_ref[:, pl.ds((g * GROUP + i) * DH, DH)].astype(F32)
             pieces.append((attn[:, cut].T * gain).astype(BF))
-        acc_out[...] += jnp.dot(
+        product = jnp.dot(
             jnp.concatenate(pieces, axis=1), w[pl.ds(g * TQ, TQ), :], preferred_element_type=F32
         )
+        if g == 0:
+            acc_out[...] = product
+        elif g < groups - 1:
+            acc_out[...] += product
+        else:
+            for j in range(4):
+                cut = slice(j * OUT, (j + 1) * OUT)
+                parts[j] = (acc_out[:, cut] + product[:, cut]).astype(BF)
 
     def largest(g, top):
         for i in range(GROUP):
@@ -319,20 +326,17 @@
     for g in range(groups):
         weigh(g, FIRST[LATE], SIZE[LATE], s_late.at[g], late_tops[g])
         finish(g)
-        if g == 2:
-            t.arrive(*[("mx", d) for d in (1, 2, 3)])
-            mx2[...] = jnp.maximum(jnp.maximum(mxbuf[...], mxgot[1]), jnp.maximum(mxgot[2], mxgot[3]))
-            for d in range(NZ):
-                t.add(("mz", d), mx2, mxgot2.at[d], device(y + 2, x, z + d, c))
-                t.start(("mz", d))
-
-    for j in range(4):
-        parts[j] = acc_out[:, pl.ds(j * OUT, OUT)].astype(BF)
+
     for i, to in reversed(list(enumerate(mates))):
         t.add(("sq", i), sqbuf, sqgot.at[i], to)
         t.add(("rs", i), parts.at[to[2]], got.at[i], to)
         t.start(("sq", i))
         t.start(("rs", i))
+    t.arrive(*[("mx", d) for d in (1, 2, 3)])
+    mx2[...] = jnp.maximum(jnp.maximum(mxbuf[...], mxgot[1]), jnp.maximum(mxgot[2], mxgot[3]))
+    for d in range(NZ):
+        t.add(("mz", d), mx2, mxgot2.at[d], device(y + 2, x, z + d, c))
+        t.start(("mz", d))
     t.arrive(*[(a, i) for i in range(3) for a in ("sq", "rs")])
     square = sqbuf[...] + sqgot[0] + sqgot[1] + sqgot[2]
     inverse = lax.rsqrt(square * (1.0 / FEATURES) + 1e-05)

time: 51.6 us -> 51 us (0.988)
  Pallas kernels: 49.7 us -> 49.1 us
    pallas_call x1, Pallas kernels: 49.7 us -> 49.1 us  [on_device(): pl.pallas_call(kernel, out_shape=(jax.ShapeDtypeStruct((ROWS, OUT), BF),...]
where the time goes in v4:
time: 51 us; the launch traced here: 50.9 us
  Pallas kernels  49.1 us (96%)
  local copies, waits for them, and re-layouts  1.14 us (2%)
  between operations  0.64 us (1%)
    pallas_call x1, Pallas kernels, on_device(): pl.pallas_call(kernel, out_shape=(jax.ShapeDtypeStruct((ROWS, OUT), BF),...  49.1 us
    unnamed x2, local copies, waits for them, and re-layouts  1.14 us

profile of v4, /device:TPU:8, one launch (start us, length us, event | category | flops | bytes accessed | tf_op | source)
XLA Modules:
  0.0 50.9 jit_solution(4147194366439891516)
XLA Ops:
  0.6 49.1 %attention.1 = (bf16[128,256]{1,0:T(8,128)(2,1)S(1)}, f32[1,16]{1,0:T(1,128)S(1)}) custom-call(s32[64]{0:T(128)} %order_hbm.1, bf16[1,2048]{1,0:T(2,128)(2,1)} %gain_hbm.1, bf16[128,2048]{1,0:T(8,128)(2,1)} %bitcast.7, bf16[128,128]{1,0:T(8,128)(2,1)} %bitcast.8, bf16[128,128]{1,0:T(8,128)(2,1)} %bitcast.9, bf16[2048,1024]{1,0:T(8,128)(2,1)} %bitcast.6), custom_call_target="tpu_custom_call" | custom-call | tf_op jit(solution)/shard_map/attention/pallas_call | solution.py:358
  49.7 0.5 %copy.10 = f32[1,16]{1,0:T(1,128)} copy(f32[1,16]{1,0:T(1,128)S(1)} %get-tuple-element.8) | data formatting | bytes 128
  50.3 0.6 %copy.11 = bf16[1,128,256]{2,1,0:T(8,128)(2,1)} copy(bf16[1,128,256]{2,1,0:T(8,128)(2,1)S(1)} %bitcast.5) | data formatting | bytes 131072

commit v5 on v4

--- a/solution.py
+++ b/solution.py
@@ -269,17 +269,23 @@
             sqbuf[...] += jnp.broadcast_to(square[:, cut], (8, ROWS))
             gain = gain_ref[:, pl.ds((g * GROUP + i) * DH, DH)].astype(F32)
             pieces.append((attn[:, cut].T * gain).astype(BF))
-        product = jnp.dot(
-            jnp.concatenate(pieces, axis=1), w[pl.ds(g * TQ, TQ), :], preferred_element_type=F32
-        )
-        if g == 0:
-            acc_out[...] = product
-        elif g < groups - 1:
-            acc_out[...] += product
-        else:
-            for j in range(4):
-                cut = slice(j * OUT, (j + 1) * OUT)
-                parts[j] = (acc_out[:, cut] + product[:, cut]).astype(BF)
+        normed = jnp.concatenate(pieces, axis=1)
+        if g < groups - 1:
+            product = jnp.dot(normed, w[pl.ds(g * TQ, TQ), :], preferred_element_type=F32)
+            acc_out[...] = product if g == 0 else acc_out[...] + product
+            return
+        for i, to in reversed(list(enumerate(mates))):
+            t.add(("sq", i), sqbuf, sqgot.at[i], to)
+            t.start(("sq", i))
+        for i, dest in ((2, mates[2][2]), (1, mates[1][2]), (0, mates[0][2]), (3, tp)):
+            cut = pl.ds(pl.multiple_of(dest * OUT, OUT), OUT)
+            product = jnp.dot(normed, w[pl.ds(g * TQ, TQ), cut], preferred_element_type=F32)
+            if i == 3:
+                acc_out[:, cut] = acc_out[:, cut] + product
+                return
+            parts[i] = (acc_out[:, cut] + product).astype(BF)
+            t.add(("rs", i), parts.at[i], got.at[i], mates[i])
+            t.start(("rs", i))
 
     def largest(g, top):
         for i in range(GROUP):
@@ -312,7 +318,6 @@
         peaks = weigh(g, FIRST[tile], SIZE[tile], buffer(n, tile), top, ahead)
         peak = peaks[0] if peaks else None
         n += 1
-    t.sent()
     late_tops = []
     for g in range(groups):
         ready(g, LATE)
@@ -327,21 +332,17 @@
         weigh(g, FIRST[LATE], SIZE[LATE], s_late.at[g], late_tops[g])
         finish(g)
 
-    for i, to in reversed(list(enumerate(mates))):
-        t.add(("sq", i), sqbuf, sqgot.at[i], to)
-        t.add(("rs", i), parts.at[to[2]], got.at[i], to)
-        t.start(("sq", i))
-        t.start(("rs", i))
     t.arrive(*[("mx", d) for d in (1, 2, 3)])
     mx2[...] = jnp.maximum(jnp.maximum(mxbuf[...], mxgot[1]), jnp.maximum(mxgot[2], mxgot[3]))
     for d in range(NZ):
         t.add(("mz", d), mx2, mxgot2.at[d], device(y + 2, x, z + d, c))
         t.start(("mz", d))
+    t.sent()
     t.arrive(*[(a, i) for i in range(3) for a in ("sq", "rs")])
     square = sqbuf[...] + sqgot[0] + sqgot[1] + sqgot[2]
     inverse = lax.rsqrt(square * (1.0 / FEATURES) + 1e-05)
     inverse = jnp.broadcast_to(inverse[:1, :], (ROWS, ROWS)).T
-    own = parts[tp].astype(F32)
+    own = acc_out[:, pl.ds(pl.multiple_of(tp * OUT, OUT), OUT)]
     result = own + got[0].astype(F32) + got[1].astype(F32) + got[2].astype(F32)
     kv_out[...] = (result * jnp.concatenate([inverse, inverse], axis=1)).astype(BF)
     t.arrive(*[("mz", d) for d in range(NZ)])
@@ -349,7 +350,6 @@
     for d in range(1, NZ):
         best = jnp.maximum(best, mxgot2[d])
     max_out[...] = best[:1, :HEADS]
-    t.sent()
 
 
 def on_device(queries, key_vectors, value_vectors, block_order, norm_gain, kv_weight):
@@ -374,7 +374,7 @@
             pltpu.VMEM((HEADS // GROUP, 1, TQ), F32),
             pltpu.VMEM((HEADS // GROUP, VROWS, TQ), F32),
             pltpu.VMEM((ROWS, COLS), F32),
-            pltpu.VMEM((4, ROWS, OUT), BF),
+            pltpu.VMEM((3, ROWS, OUT), BF),
             pltpu.VMEM((3, ROWS, OUT), BF),
             pltpu.VMEM((8, DH), F32),
             pltpu.VMEM((3, 8, DH), F32),

time: 51 us -> 50.8 us (level)
  no operation moved by 1% of the time
where the time goes in v5:
time: 50.8 us; the launch traced here: 50.7 us
  Pallas kernels  48.9 us (96%)
  local copies, waits for them, and re-layouts  1.14 us (2%)
  between operations  0.64 us (1%)
    pallas_call x1, Pallas kernels, on_device(): pl.pallas_call(kernel, out_shape=(jax.ShapeDtypeStruct((ROWS, OUT), BF),...  48.9 us
    unnamed x2, local copies, waits for them, and re-layouts  1.14 us

profile of v5, /device:TPU:8, one launch (start us, length us, event | category | flops | bytes accessed | tf_op | source)
XLA Modules:
  0.0 50.7 jit_solution(4202489924686540127)
XLA Ops:
  0.6 48.9 %attention.1 = (bf16[128,256]{1,0:T(8,128)(2,1)S(1)}, f32[1,16]{1,0:T(1,128)S(1)}) custom-call(s32[64]{0:T(128)} %order_hbm.1, bf16[1,2048]{1,0:T(2,128)(2,1)} %gain_hbm.1, bf16[128,2048]{1,0:T(8,128)(2,1)} %bitcast.7, bf16[128,128]{1,0:T(8,128)(2,1)} %bitcast.8, bf16[128,128]{1,0:T(8,128)(2,1)} %bitcast.9, bf16[2048,1024]{1,0:T(8,128)(2,1)} %bitcast.6), custom_call_target="tpu_custom_call" | custom-call | tf_op jit(solution)/shard_map/attention/pallas_call | solution.py:358
  49.6 0.5 %copy.10 = f32[1,16]{1,0:T(1,128)} copy(f32[1,16]{1,0:T(1,128)S(1)} %get-tuple-element.8) | data formatting | bytes 128
  50.1 0.6 %copy.11 = bf16[1,128,256]{2,1,0:T(8,128)(2,1)} copy(bf16[1,128,256]{2,1,0:T(8,128)(2,1)S(1)} %bitcast.5) | data formatting | bytes 131072

commit v6 on v5

--- a/solution.py
+++ b/solution.py
@@ -120,12 +120,6 @@
     pp, cp, tp = lax.axis_index("pp"), lax.axis_index("cp"), lax.axis_index("tp")
     y, x, z, c = pp * 2 + tp // 2, cp // NZ, cp % NZ, tp % 2
 
-    vcopy = pltpu.make_async_copy(v_hbm, vin, local.at[1])
-    vcopy.start()
-    ocopy = pltpu.make_async_copy(order_hbm, order, local.at[2])
-    ocopy.start()
-    gcopy = pltpu.make_async_copy(gain_hbm, gain_ref, local.at[3])
-    gcopy.start()
     barrier = pltpu.get_barrier_semaphore()
     peers = [device(y, x + d, z, c) for d in (1, 2, 3)]
     peers += [device(y, x, z + d, c) for d in (1, 7)]
@@ -134,13 +128,14 @@
     mates = [device(y, x, z, 1 - c), device(other, x, z, c), device(other, x, z, 1 - c)]
     for d in peers + mates:
         pl.semaphore_signal(barrier, inc=1, device_id=d, device_id_type=MESH)
+    vcopy = pltpu.make_async_copy(v_hbm, vin, local.at[1])
+    vcopy.start()
+    ocopy = pltpu.make_async_copy(order_hbm, order, local.at[2])
+    ocopy.start()
+    gcopy = pltpu.make_async_copy(gain_hbm, gain_ref, local.at[3])
+    gcopy.start()
     wcopy = pltpu.make_async_copy(w_hbm, w, local.at[0])
     wcopy.start()
-
-    vcopy.wait()
-    ocopy.wait()
-    gcopy.wait()
-    vown[...] = vin[...].astype(F32).T.astype(BF)
 
     t = Traffic(send, recv)
 
@@ -187,8 +182,15 @@
 
     pl.semaphore_wait(barrier, len(peers) + len(mates))
 
-    for name in ["k", "v"] + [("q", h) for h in range(HEADS)]:
-        t.start(name)
+    t.start("k")
+    t.start(("q", 0))
+    vcopy.wait()
+    vown[...] = vin[...].astype(F32).T.astype(BF)
+    t.start("v")
+    for h in range(1, HEADS):
+        t.start(("q", h))
+    ocopy.wait()
+    gcopy.wait()
 
     row = lax.broadcasted_iota(jnp.int32, (ROWS, DH), 0)
     lane = lax.broadcasted_iota(jnp.int32, (ROWS, DH), 1)

time: 50.8 us -> 50.8 us (level)
  no operation moved by 1% of the time
where the time goes in v6:
time: 50.8 us; the launch traced here: 50.7 us
  Pallas kernels  48.9 us (96%)
  local copies, waits for them, and re-layouts  1.14 us (2%)
  between operations  0.64 us (1%)
    pallas_call x1, Pallas kernels, on_device(): pl.pallas_call(kernel, out_shape=(jax.ShapeDtypeStruct((ROWS, OUT), BF),...  48.9 us
    unnamed x2, local copies, waits for them, and re-layouts  1.14 us

profile of v6, /device:TPU:8, one launch (start us, length us, event | category | flops | bytes accessed | tf_op | source)
XLA Modules:
  0.0 50.7 jit_solution(13953074543954310263)
XLA Ops:
  0.6 48.9 %attention.1 = (bf16[128,256]{1,0:T(8,128)(2,1)S(1)}, f32[1,16]{1,0:T(1,128)S(1)}) custom-call(s32[64]{0:T(128)} %order_hbm.1, bf16[1,2048]{1,0:T(2,128)(2,1)} %gain_hbm.1, bf16[128,2048]{1,0:T(8,128)(2,1)} %bitcast.7, bf16[128,128]{1,0:T(8,128)(2,1)} %bitcast.8, bf16[128,128]{1,0:T(8,128)(2,1)} %bitcast.9, bf16[2048,1024]{1,0:T(8,128)(2,1)} %bitcast.6), custom_call_target="tpu_custom_call" | custom-call | tf_op jit(solution)/shard_map/attention/pallas_call | solution.py:360
  49.6 0.5 %copy.10 = f32[1,16]{1,0:T(1,128)} copy(f32[1,16]{1,0:T(1,128)S(1)} %get-tuple-element.8) | data formatting | bytes 128
  50.1 0.6 %copy.11 = bf16[1,128,256]{2,1,0:T(8,128)(2,1)} copy(bf16[1,128,256]{2,1,0:T(8,128)(2,1)S(1)} %bitcast.5) | data formatting | bytes 131072

commit v7 on v5

--- a/solution.py
+++ b/solution.py
@@ -52,10 +52,10 @@
     + [("arrive", ("vz", 1), ("vz", -1)), ring(0, 0)]
     + [(0, 0), ("flush",), ring(0, 1, 3, 2), ("arrive", ("vz", 2), ("vz", -2)), ring(1, 0)]
     + [(1, 0), (0, 1), (1, 1), (2, 0), (2, 1), ("arrive", ("vz", 3), ("vz", -3))]
-    + [(0, 2), ring(1, 1, 3), (1, 2), ring(1, 2)]
-    + [(2, 2), ring(2, 0), (3, 0), (3, 1), ("arrive", ("vz", 4), ("vz", -4))]
-    + [(3, 2), (0, 3), ring(2, 1, 3), (1, 3), ring(2, 2)]
-    + [(2, 3), (3, 3), (0, 4), (1, 4), (2, 4), (3, 4), ("flush",)]
+    + [(0, 2), (1, 2), ring(1, 1, 3), (2, 2), ring(1, 2)]
+    + [ring(2, 0), (3, 0), (3, 1), ("arrive", ("vz", 4), ("vz", -4))]
+    + [(3, 2), (0, 3), (1, 3), ring(2, 1, 3)]
+    + [(2, 3), ring(2, 2), (3, 3), (0, 4), (1, 4), (2, 4), (3, 4), ("flush",)]
 )
 
 

time: 50.8 us -> 50.4 us (level)
  no operation moved by 1% of the time
where the time goes in v7:
time: 50.4 us; the launch traced here: 50.3 us
  Pallas kernels  48.5 us (96%)
  local copies, waits for them, and re-layouts  1.14 us (2%)
  between operations  0.64 us (1%)
    pallas_call x1, Pallas kernels, on_device(): pl.pallas_call(kernel, out_shape=(jax.ShapeDtypeStruct((ROWS, OUT), BF),...  48.5 us
    unnamed x2, local copies, waits for them, and re-layouts  1.14 us

profile of v7, /device:TPU:8, one launch (start us, length us, event | category | flops | bytes accessed | tf_op | source)
XLA Modules:
  0.0 50.3 jit_solution(6864877714810579288)
XLA Ops:
  0.6 48.5 %attention.1 = (bf16[128,256]{1,0:T(8,128)(2,1)S(1)}, f32[1,16]{1,0:T(1,128)S(1)}) custom-call(s32[64]{0:T(128)} %order_hbm.1, bf16[1,2048]{1,0:T(2,128)(2,1)} %gain_hbm.1, bf16[128,2048]{1,0:T(8,128)(2,1)} %bitcast.7, bf16[128,128]{1,0:T(8,128)(2,1)} %bitcast.8, bf16[128,128]{1,0:T(8,128)(2,1)} %bitcast.9, bf16[2048,1024]{1,0:T(8,128)(2,1)} %bitcast.6), custom_call_target="tpu_custom_call" | custom-call | tf_op jit(solution)/shard_map/attention/pallas_call | solution.py:358
  49.1 0.5 %copy.10 = f32[1,16]{1,0:T(1,128)} copy(f32[1,16]{1,0:T(1,128)S(1)} %get-tuple-element.8) | data formatting | bytes 128
  49.6 0.6 %copy.11 = bf16[1,128,256]{2,1,0:T(8,128)(2,1)} copy(bf16[1,128,256]{2,1,0:T(8,128)(2,1)S(1)} %bitcast.5) | data formatting | bytes 131072
